TPU v7x, 32 devices: a whole 2x2x4 slice. The times are simulated.
32 devices in a mesh: section: 2 (over y), seq: 4 (over x, core), rep: 4 (over z).
Axes of the slice: x: 2, y: 2, z: 4, core: 2. Of those that a mesh axis runs over, the one named last changes fastest.
Arguments:
- inputs: bfloat16 [2, 4, 512, 1152], P(None, 'rep', 'seq', 'section'), may hold values from -6 to 6
- w_query: bfloat16 [2, 1152, 1152], P('section', 'seq'), may hold values from -0.1875 to 0.1875
- w_key: bfloat16 [2, 1152, 384], P('section', 'seq'), may hold values from -0.1875 to 0.1875
- w_value: bfloat16 [2, 1152, 384], P('section', 'seq'), may hold values from -0.1875 to 0.1875
- w_out: bfloat16 [2, 1152, 1152], P('section', 'seq'), may hold values from -1.5 to 1.5
- w_gate: bfloat16 [2, 1152, 3072], P('section', 'seq'), may hold values from -0.1875 to 0.1875
- w_up: bfloat16 [2, 1152, 3072], P('section', 'seq'), may hold values from -0.1875 to 0.1875
- w_down: bfloat16 [2, 3072, 1152], P('section', 'seq'), may hold values from -0.109375 to 0.109375
- norm_attn: bfloat16 [2, 1152], P('section', 'seq'), may hold values from 0.5 to 1.5
- norm_ffn: bfloat16 [2, 1152], P('section', 'seq'), may hold values from 0.5 to 1.5
- image_start: int32 [2, 4], P(None, 'rep'), may hold values from 0 to 256, as said below
- cotangent: bfloat16 [2, 4, 512, 1152], P(None, 'rep', 'seq', 'section'), may hold values from -6 to 6
Outputs:
- block_out: float32 [2, 4, 512, 1152], P(None, 'rep', 'seq', 'section')
- input_grad: float32 [2, 4, 512, 1152], P(None, 'rep', 'seq', 'section')
- grad_query: float32 [2, 1152, 1152], P('section', 'seq')
- grad_key: float32 [2, 1152, 384], P('section', 'seq')
- grad_value: float32 [2, 1152, 384], P('section', 'seq')
- grad_out: float32 [2, 1152, 1152], P('section', 'seq')
- grad_gate: float32 [2, 1152, 3072], P('section', 'seq')
- grad_up: float32 [2, 1152, 3072], P('section', 'seq')
- grad_down: float32 [2, 3072, 1152], P('section', 'seq')
- grad_norm_attn: float32 [2, 1152], P('section', 'seq')
- grad_norm_ffn: float32 [2, 1152], P('section', 'seq')
Inputs may be any that keep to these rules, and one draw needn't show every extreme that they name: `image_start`: each sequence's image span starts at a multiple of 256 and lies inside the sequence.
All inputs are finite; a program needn't handle non-finite values.
Results may differ from a plain program's by a relative error of at most 0.025.
Values may be sent and summed in bfloat16 or wider, within the bound.
No kernel may reach another device: no remote copies, remote signals or barrier semaphores. Data moves between devices by JAX's collectives and lax.ppermute only.
A program may use at most 256 MiB of HBM per device.

v0:
```python
import jax
import jax.numpy as jnp
from jax import lax
from jax.experimental import pallas as pl
from jax.experimental.pallas import tpu as pltpu
from jax.sharding import PartitionSpec as P

HQ = 18
KVH = 6
DH = 64
IMG = 256
GROUP = HQ // KVH
PAIRS = KVH // 2
QT = 2 * GROUP * DH
KT = 2 * DH
WQ = HQ * DH
WK = KVH * DH
masked_value = -1e30
F32 = jnp.float32
BF16 = jnp.bfloat16


def flip(block, bit, axis="seq"):
    return lax.ppermute(block, axis, [(i, i ^ bit) for i in range(lax.axis_size(axis))])


def shifted(block, axis, distance):
    devices = range(lax.axis_size(axis))
    route = [(i - distance, i) for i in devices if i - distance in devices]
    return lax.ppermute(block, axis, route)


def bits_below(count):
    return [1 << i for i in range(count.bit_length() - 1)]


def flip_gather(block, count):
    held = {0: block}
    for bit in reversed(bits_below(count)):
        held.update({p | bit: flip(piece, bit) for p, piece in list(held.items())})
    return [held[p] for p in range(count)]


def flip_reduce(pieces, count):
    held = dict(enumerate(pieces))
    for bit in bits_below(count):
        kept = [p for p in held if not p & bit]
        last = 2 * bit == count
        added = {p: flip(held[p | bit], bit) for p in kept}
        if last:
            return held[0], added[0]
        held = {p: held[p] + added[p] for p in kept}


def put_rows(pieces, places):
    whole = jnp.zeros((len(pieces),) + pieces[0].shape, pieces[0].dtype)
    for place, piece in zip(places, pieces):
        whole = lax.dynamic_update_slice(whole, piece[None], (place,) + (0,) * piece.ndim)
    return whole.reshape((len(pieces) * pieces[0].shape[0],) + pieces[0].shape[1:])


def gather_rows(shard, count, me):
    pieces = flip_gather(shard, count)
    return put_rows(pieces, [me ^ p for p in range(count)])


def gather_over_rep(shard, count, me):
    reps = lax.axis_size("rep")
    if count != 4 or shard.shape[0] % (8 * reps):
        return gather_rows(shard, count, me)
    here = lax.axis_index("rep")
    depth = shard.shape[0] // reps
    part = flip(lax.dynamic_slice_in_dim(shard, here * depth, depth, 0), 2)
    parts = [part] + [
        lax.ppermute(part, "rep", [(i, (i + k) % reps) for i in range(reps)])
        for k in range(1, reps)
    ]
    across = put_rows(parts, [(here - k) % reps for k in range(reps)])
    pieces = [shard, flip(shard, 1), across, flip(across, 1)]
    return put_rows(pieces, [me ^ p for p in range(count)])


def rep_sum(value):
    count = lax.axis_size("rep")
    if count != 4:
        return lax.psum(value, "rep").astype(BF16)
    here = lax.axis_index("rep")
    inner = (here == 1) | (here == 2)
    value = value + lax.ppermute(value, "rep", [(0, 1), (3, 2)])
    value = value + lax.ppermute(value, "rep", [(1, 2), (2, 1)])
    arrived = lax.ppermute(value, "rep", [(1, 0), (2, 3)])
    return jnp.where(inner, value, arrived)


def dot_nn(left, right):
    return jnp.dot(left, right, preferred_element_type=F32)


def dot_nt(left, right):
    return lax.dot_general(left, right, (((1,), (1,)), ((), ())), preferred_element_type=F32)


def inverse_rms(hidden):
    return lax.rsqrt(jnp.mean(hidden * hidden, axis=-1, keepdims=True) + 1e-05)


def kernel(body, flops, size, **options):
    cost = pl.CostEstimate(flops=flops, bytes_accessed=size, transcendentals=0)
    return pl.pallas_call(body, cost_estimate=cost, **options)


def shape_of(rows, cols, kind=BF16):
    return jax.ShapeDtypeStruct((rows, cols), kind)


def fixed(*extent):
    return pl.BlockSpec(extent, lambda *step: (0,) * len(extent))


def other_half(tile):
    lane = lax.broadcasted_iota(jnp.int32, tile.shape, 1)
    low = lane % DH < DH // 2
    return jnp.where(low, pltpu.roll(tile, KT - DH // 2, 1), pltpu.roll(tile, DH // 2, 1))


def project_kernel(h_ref, gain_ref, w_ref, cos_ref, sin_ref, normed_ref, q_ref, kv_ref):
    step = pl.program_id(0)

    @pl.when(step == 0)
    def _():
        hidden = h_ref[...].astype(F32)
        normed_ref[...] = (hidden * inverse_rms(hidden) * gain_ref[...]).astype(BF16)

    product = dot_nn(normed_ref[...], w_ref[...])

    def turned(scale, out_ref):
        for start in range(0, WK, KT):
            tile = product[:, start : start + KT]
            result = tile * cos_ref[...] + other_half(tile) * sin_ref[...]
            out_ref[:, start : start + KT] = (result * scale).astype(BF16)

    @pl.when(step < GROUP)
    def _():
        turned(DH ** (-0.5), q_ref)

    @pl.when(step == GROUP)
    def _():
        turned(1.0, kv_ref)

    @pl.when(step == GROUP + 1)
    def _():
        kv_ref[...] = product.astype(BF16)


def project(hidden, gain, w_qkv, cosine, sine):
    rows, model = hidden.shape
    return kernel(
        project_kernel,
        2 * rows * w_qkv.size,
        2 * w_qkv.size + 8 * hidden.size,
        grid=(GROUP + 2,),
        in_specs=[
            fixed(rows, model),
            fixed(1, model),
            pl.BlockSpec((model, WK), lambda j: (0, j)),
            fixed(rows, KT),
            fixed(rows, KT),
        ],
        out_specs=[
            fixed(rows, model),
            pl.BlockSpec((rows, WK), lambda j: (0, jnp.minimum(j, GROUP - 1))),
            pl.BlockSpec((rows, WK), lambda j: (0, jnp.maximum(j - GROUP, 0))),
        ],
        out_shape=(shape_of(rows, model), shape_of(rows, WQ), shape_of(rows, 2 * WK)),
    )(hidden, gain, w_qkv, cosine, sine)


def attend_kernel(q_ref, k_ref, v_ref, bias_ref, o_ref, lse_ref):
    bias = bias_ref[...]
    values_t = v_ref[...].T
    for tile in range(GROUP):
        queries_t = q_ref[:, tile * KT : (tile + 1) * KT].T
        outs = []
        for half in range(2):
            head = 2 * tile + half
            kv = head // GROUP
            keys = k_ref[:, kv * DH : (kv + 1) * DH]
            logits = dot_nn(keys, queries_t[half * DH : (half + 1) * DH]) + bias
            top = jnp.max(logits, axis=0, keepdims=True)
            exponent = jnp.exp(logits - top)
            total = jnp.sum(exponent, axis=0, keepdims=True)
            attend = (exponent * (1.0 / total)).astype(BF16)
            outs.append(dot_nn(values_t[kv * DH : (kv + 1) * DH], attend))
            lse_ref[0, head : head + 1, :] = top + jnp.log(total)
        joined = jnp.concatenate(outs, axis=0).T
        o_ref[:, tile * KT : (tile + 1) * KT] = joined.astype(BF16)


def attend_forward(queries, keys_values, bias):
    rows, length = queries.shape[0], keys_values.shape[0]
    count = HQ * rows * length
    return kernel(
        attend_kernel,
        count * 8 * DH,
        4 << 20,
        grid=(PAIRS,),
        in_specs=[
            pl.BlockSpec((rows, QT), lambda i: (0, i)),
            pl.BlockSpec((length, KT), lambda i: (0, i)),
            pl.BlockSpec((length, KT), lambda i: (0, i + PAIRS)),
            fixed(length, rows),
        ],
        out_specs=[
            pl.BlockSpec((rows, QT), lambda i: (0, i)),
            pl.BlockSpec((1, 8, rows), lambda i: (i, 0, 0)),
        ],
        out_shape=(shape_of(rows, WQ), jax.ShapeDtypeStruct((PAIRS, 8, rows), F32)),
    )(queries, keys_values, keys_values, bias)


def attend_back_kernel(
    q_ref, k_ref, v_ref, do_ref, bias_ref, lse_ref, cos_ref, sin_ref, dq_ref, *dkv_refs
):
    bias = bias_ref[...]
    keys_t = k_ref[...].T
    dk = [None, None]
    dv = [None, None]
    for tile in range(GROUP):
        q_tile = q_ref[:, tile * KT : (tile + 1) * KT]
        do_tile = do_ref[:, tile * KT : (tile + 1) * KT]
        queries_t = q_tile.T
        do_t = do_tile.T
        grads = []
        for half in range(2):
            head = 2 * tile + half
            kv = head // GROUP
            span = slice(half * DH, (half + 1) * DH)
            kv_span = slice(kv * DH, (kv + 1) * DH)
            logits = dot_nn(k_ref[:, kv_span], queries_t[span]) + bias
            attend = jnp.exp(logits - lse_ref[0, head : head + 1, :])
            d_attend = dot_nn(v_ref[:, kv_span], do_t[span])
            delta = jnp.sum(d_attend * attend, axis=0, keepdims=True)
            d_scores = (attend * (d_attend - delta)).astype(BF16)
            grads.append(dot_nn(keys_t[kv_span], d_scores))
            dk_term = dot_nn(d_scores, q_tile[:, span])
            dv_term = dot_nn(attend.astype(BF16), do_tile[:, span])
            dk[kv] = dk_term if dk[kv] is None else dk[kv] + dk_term
            dv[kv] = dv_term if dv[kv] is None else dv[kv] + dv_term
        joined = jnp.concatenate(grads, axis=0).T * DH ** (-0.5)
        turned = joined * cos_ref[...] - other_half(joined) * sin_ref[...]
        dq_ref[:, tile * KT : (tile + 1) * KT] = turned.astype(BF16)
    d_keys = jnp.concatenate(dk, axis=1).astype(BF16)
    d_values = jnp.concatenate(dv, axis=1).astype(BF16)
    rows = dq_ref.shape[0]
    for p in range(len(dkv_refs) // 2):
        dkv_refs[2 * p][...] = d_keys[p * rows : (p + 1) * rows]
        dkv_refs[2 * p + 1][...] = d_values[p * rows : (p + 1) * rows]


def attend_backward(queries, keys_values, d_mixed, bias, lse, cosine, sine):
    rows, length = queries.shape[0], keys_values.shape[0]
    count = HQ * rows * length
    narrow = pl.BlockSpec((rows, KT), lambda i: (0, i))
    total = 2 * (length // rows)
    return kernel(
        attend_back_kernel,
        count * 16 * DH,
        8 << 20,
        grid=(PAIRS,),
        in_specs=[
            pl.BlockSpec((rows, QT), lambda i: (0, i)),
            pl.BlockSpec((length, KT), lambda i: (0, i)),
            pl.BlockSpec((length, KT), lambda i: (0, i + PAIRS)),
            pl.BlockSpec((rows, QT), lambda i: (0, i)),
            fixed(length, rows),
            pl.BlockSpec((1, 8, rows), lambda i: (i, 0, 0)),
            fixed(rows, KT),
            fixed(rows, KT),
        ],
        out_specs=[pl.BlockSpec((rows, QT), lambda i: (0, i))] + [narrow] * total,
        out_shape=(shape_of(rows, WQ),) + (shape_of(rows, WK),) * total,
    )(queries, keys_values, keys_values, d_mixed, bias, lse, cosine, sine)


def mix_kernel(mixed_ref, w_ref, h_ref, gain_ref, middle_ref, ffn_ref):
    step = pl.program_id(0)

    @pl.when(step == 0)
    def _():
        middle_ref[...] = h_ref[...].astype(F32)

    middle_ref[...] += dot_nn(mixed_ref[...], w_ref[...])

    @pl.when(step == pl.num_programs(0) - 1)
    def _():
        middle = middle_ref[...]
        ffn_ref[...] = (middle * inverse_rms(middle) * gain_ref[...]).astype(BF16)


def mix(mixed, w_out, hidden, gain):
    rows, model = hidden.shape
    tile = WK
    return kernel(
        mix_kernel,
        2 * rows * w_out.size,
        2 * w_out.size + 8 * hidden.size,
        grid=(WQ // tile,),
        in_specs=[
            pl.BlockSpec((rows, tile), lambda j: (0, j)),
            pl.BlockSpec((tile, model), lambda j: (j, 0)),
            fixed(rows, model),
            fixed(1, model),
        ],
        out_specs=[fixed(rows, model), fixed(rows, model)],
        out_shape=(shape_of(rows, model, F32), shape_of(rows, model)),
    )(mixed, w_out, hidden, gain)


def gate_kernel(x_ref, wg_ref, wu_ref, inner_ref, *slope_refs):
    gate = dot_nn(x_ref[...], wg_ref[...])
    up = dot_nn(x_ref[...], wu_ref[...])
    sig = 1.0 / (1.0 + jnp.exp(-gate))
    silu = gate * sig
    inner_ref[...] = (silu * up).astype(BF16)
    if slope_refs:
        slope_refs[0][...] = (up * (sig * (1.0 + gate * (1.0 - sig)))).astype(BF16)
        slope_refs[1][...] = silu.astype(BF16)


def gate_up(ffn_in, w_gate, w_up, slopes):
    rows, model = ffn_in.shape
    width = w_gate.shape[1]
    tile = width // 4
    outs = 3 if slopes else 1
    cols = pl.BlockSpec((rows, tile), lambda j: (0, j))
    weight = pl.BlockSpec((model, tile), lambda j: (0, j))
    return kernel(
        gate_kernel,
        4 * rows * w_gate.size,
        4 * w_gate.size + 2 * outs * rows * width,
        grid=(width // tile,),
        in_specs=[fixed(rows, model), weight, weight],
        out_specs=[cols] * outs,
        out_shape=(shape_of(rows, width),) * outs,
    )(ffn_in, w_gate, w_up)


def down_kernel(inner_ref, w_ref, middle_ref, out_ref, low_ref):
    step = pl.program_id(0)

    @pl.when(step == 0)
    def _():
        out_ref[...] = middle_ref[...]

    out_ref[...] += dot_nn(inner_ref[...], w_ref[...])

    @pl.when(step == pl.num_programs(0) - 1)
    def _():
        low_ref[...] = out_ref[...].astype(BF16)


def down(inner, w_down, middle):
    rows, model = middle.shape
    width = w_down.shape[0]
    tile = width // 4
    return kernel(
        down_kernel,
        2 * rows * w_down.size,
        2 * w_down.size + 12 * middle.size,
        grid=(width // tile,),
        in_specs=[
            pl.BlockSpec((rows, tile), lambda j: (0, j)),
            pl.BlockSpec((tile, model), lambda j: (j, 0)),
            fixed(rows, model),
        ],
        out_specs=[fixed(rows, model), fixed(rows, model)],
        out_shape=(shape_of(rows, model, F32), shape_of(rows, model)),
    )(inner, w_down, middle)


def d_inner_kernel(g_ref, w_ref, gate_slope_ref, up_slope_ref, out_ref):
    d_inner = dot_nt(g_ref[...], w_ref[...])
    out_ref[0] = (d_inner * gate_slope_ref[...].astype(F32)).astype(BF16)
    out_ref[1] = (d_inner * up_slope_ref[...].astype(F32)).astype(BF16)


def d_inner(grad, w_down, gate_slope, up_slope):
    rows, model = grad.shape
    width = w_down.shape[0]
    tile = width // 4
    cols = pl.BlockSpec((rows, tile), lambda j: (0, j))
    return kernel(
        d_inner_kernel,
        2 * rows * w_down.size,
        2 * w_down.size + 8 * rows * width,
        grid=(width // tile,),
        in_specs=[
            fixed(rows, model),
            pl.BlockSpec((tile, model), lambda j: (j, 0)),
            cols,
            cols,
        ],
        out_specs=pl.BlockSpec((2, rows, tile), lambda j: (0, 0, j)),
        out_shape=jax.ShapeDtypeStruct((2, rows, width), BF16),
    )(grad, w_down, gate_slope, up_slope)


def norm_back(hidden, gain, d_normed):
    inverse = inverse_rms(hidden)
    scaled = d_normed * gain
    mean = jnp.mean(scaled * hidden, axis=-1, keepdims=True)
    back = inverse * (scaled - hidden * (inverse * inverse) * mean)
    return back, jnp.sum(d_normed * hidden * inverse, axis=0, keepdims=True)


def d_middle_kernel(
    d_ref, wg_ref, wu_ref, middle_ref, gain_ref, g_ref, wo_ref,
    dm_ref, low_ref, mixed_ref, gain_grad_ref, total,
):
    step = pl.program_id(0)
    half = pl.num_programs(0) // 2

    @pl.when(step == 0)
    def _():
        total[...] = jnp.zeros_like(total)

    @pl.when(step < half)
    def _():
        total[...] += dot_nt(d_ref[0], wg_ref[...])

    @pl.when(step >= half)
    def _():
        total[...] += dot_nt(d_ref[0], wu_ref[...])

    @pl.when(step == pl.num_programs(0) - 1)
    def _():
        back, gain_grad = norm_back(middle_ref[...], gain_ref[...], total[...])
        d_middle = g_ref[...].astype(F32) + back
        dm_ref[...] = d_middle
        low = d_middle.astype(BF16)
        low_ref[...] = low
        mixed_ref[...] = dot_nt(low, wo_ref[...]).astype(BF16)
        gain_grad_ref[...] = gain_grad


def d_middle(d_gu, w_gate, w_up, middle, gain, grad, w_out):
    rows, model = middle.shape
    width = w_gate.shape[1]
    tile = width // 2
    half = width // tile
    return kernel(
        d_middle_kernel,
        4 * rows * w_gate.size + 2 * rows * w_out.size,
        4 * w_gate.size + 4 * rows * width + 12 * middle.size,
        grid=(2 * half,),
        in_specs=[
            pl.BlockSpec((1, rows, tile), lambda j: (j // half, 0, j % half)),
            pl.BlockSpec((model, tile), lambda j: (0, jnp.minimum(j, half - 1))),
            pl.BlockSpec((model, tile), lambda j: (0, jnp.maximum(j - half, 0))),
            fixed(rows, model),
            fixed(1, model),
            fixed(rows, model),
            fixed(*w_out.shape),
        ],
        out_specs=[fixed(rows, model)] * 2 + [fixed(rows, WQ), fixed(1, model)],
        out_shape=(
            shape_of(rows, model, F32),
            shape_of(rows, model),
            shape_of(rows, WQ),
            shape_of(1, model, F32),
        ),
        scratch_shapes=[pltpu.VMEM((rows, model), F32)],
    )(d_gu, w_gate, w_up, middle, gain, grad, w_out)


def d_hidden_kernel(
    dq_ref, dk_ref, dv_ref, dk2_ref, dv2_ref, cos_ref, sin_ref, w_ref, h_ref, gain_ref, dm_ref,
    dkv_ref, dh_ref, low_ref, gain_grad_ref,
):
    for start in range(0, WK, KT):
        tile = dk_ref[:, start : start + KT].astype(F32)
        tile += dk2_ref[:, start : start + KT].astype(F32)
        turned = tile * cos_ref[...] - other_half(tile) * sin_ref[...]
        dkv_ref[:, start : start + KT] = turned.astype(BF16)
    dkv_ref[:, WK:] = (dv_ref[...].astype(F32) + dv2_ref[...].astype(F32)).astype(BF16)
    d_normed = dot_nt(dq_ref[...], w_ref[:, :WQ]) + dot_nt(dkv_ref[...], w_ref[:, WQ:])
    back, gain_grad = norm_back(h_ref[...].astype(F32), gain_ref[...], d_normed)
    d_hidden = dm_ref[...] + back
    dh_ref[...] = d_hidden
    low_ref[...] = d_hidden.astype(BF16)
    gain_grad_ref[...] = gain_grad


def d_hidden(dq, dkv, cosine, sine, w_qkv, hidden, gain, d_mid):
    rows, model = hidden.shape
    return kernel(
        d_hidden_kernel,
        2 * rows * w_qkv.size,
        2 * w_qkv.size + 16 * hidden.size,
        out_shape=(
            shape_of(rows, 2 * WK),
            shape_of(rows, model, F32),
            shape_of(rows, model),
            shape_of(1, model, F32),
        ),
    )(dq, *dkv, cosine, sine, w_qkv, hidden, gain, d_mid)


def forward_layer(hidden, weights, place, tick):
    w_qkv, w_out, w_gate, w_up, w_down, gain_attn, gain_ffn = weights
    group, cosine, sine, bias = place
    normed, queries, kv_own = project(hidden, gain_attn, w_qkv, cosine, sine)
    kv_all = jnp.concatenate(flip_gather(kv_own, group), axis=0)
    mixed, lse = attend_forward(queries, kv_all, bias)
    middle, ffn_in = mix(mixed, w_out, hidden, gain_ffn)
    inner, *slopes = gate_up(ffn_in, w_gate, w_up, tick != "a")
    out, low = down(inner, w_down, middle)
    return out, low, (hidden, normed, queries, kv_all, lse, mixed, middle, ffn_in, inner, slopes)


def backward_layer(grad, kept, weights, place):
    w_qkv, w_out, w_gate, w_up, w_down, gain_attn, gain_ffn = weights
    group, cosine, sine, bias = place
    hidden, normed, queries, kv_all, lse, mixed, middle, ffn_in, inner, slopes = kept
    d_gu = d_inner(grad, w_down, *slopes)
    d_mid, mid_low, d_mixed, gain_ffn_grad = d_middle(
        d_gu, w_gate, w_up, middle, gain_ffn, grad, w_out
    )
    d_q, *d_kv = attend_backward(queries, kv_all, d_mixed, bias, lse, cosine, sine)
    dk, dk2 = flip_reduce(d_kv[0::2], group)
    dv, dv2 = flip_reduce(d_kv[1::2], group)
    d_kv, d_hid, hid_low, gain_attn_grad = d_hidden(
        d_q, (dk, dv, dk2, dv2), cosine, sine, w_qkv, hidden, gain_attn, d_mid
    )
    pairs = {
        "d": (inner, (grad,)),
        "g": (ffn_in, (d_gu,)),
        "o": (mixed, (mid_low,)),
        "q": (normed, (d_q, d_kv)),
    }
    return d_hid, hid_low, pairs, (gain_attn_grad, gain_ffn_grad)


def grad_kernel(*refs):
    total = (len(refs) - 2) // 3
    for lefts, out in ((refs[:total], refs[-2]), (refs[total : 2 * total], refs[-1])):
        product = None
        for left, right in zip(lefts, refs[2 * total : 3 * total]):
            operand = right[0] if len(right.shape) == 3 else right[...]
            term = dot_nn(left[...], operand)
            product = term if product is None else product + term
        out[...] = product.astype(BF16)


def grad_product(lefts, rights, depth, row, rows, plane, col, cols, tile_cols):
    tokens = rights[0].shape[-2]
    first_col = col // tile_cols
    left = lambda base: pl.BlockSpec((rows, tokens), lambda j: (base, 0))
    if rights[0].ndim == 3:
        right = pl.BlockSpec((1, tokens, tile_cols), lambda j: (plane, 0, first_col + j))
    else:
        right = pl.BlockSpec((tokens, tile_cols), lambda j: (0, first_col + j))
    out = pl.BlockSpec((rows, tile_cols), lambda j: (0, j))
    total = len(lefts)
    return kernel(
        grad_kernel,
        4 * total * tokens * rows * cols,
        8 * rows * cols,
        grid=(cols // tile_cols,),
        in_specs=[left((depth + row) // rows)] * total + [left(row // rows)] * total + [right] * total,
        out_specs=[out, out],
        out_shape=(shape_of(rows, cols), shape_of(rows, cols)),
    )(*lefts, *lefts, *rights)


def left_rows(left, me, count, group):
    left_t = left.T
    depth = left_t.shape[0] // count

    def rows_of(p):
        first = lax.dynamic_slice_in_dim(left_t, (me ^ p) * depth, depth, 0)
        second = lax.dynamic_slice_in_dim(left_t, (me ^ p ^ group) * depth, depth, 0)
        return jnp.concatenate([first, second], axis=0)

    return [rows_of(0)] + [flip(rows_of(p), p) for p in range(1, group)]


def right_rows(right, group):
    return [right] + [flip(right, p) for p in range(1, group)]


def reduced(other, own, group):
    return rep_sum(own + flip(other, group))


def shards(
    inputs,
    w_query,
    w_key,
    w_value,
    w_out,
    w_gate,
    w_up,
    w_down,
    norm_attn,
    norm_ffn,
    image_start,
    cotangent,
):
    is_first = lax.axis_index("section") == 0
    me = lax.axis_index("seq")
    count = lax.axis_size("seq")
    micro_count, _, piece_rows, half_width = inputs.shape
    group = count // micro_count
    micro = me // group
    own_input = inputs[:, 0]
    own_cotan = cotangent[:, 0]
    incoming = flip(jnp.where(is_first, own_cotan, own_input), 1, "section")
    whole = jnp.where(
        is_first,
        jnp.concatenate([own_input, incoming], axis=-1),
        jnp.concatenate([incoming, own_cotan], axis=-1),
    )
    kept_block = lax.dynamic_index_in_dim(whole, micro, 0, keepdims=False)
    sent_block = lax.dynamic_index_in_dim(whole, 1 - micro, 0, keepdims=False)
    given = jnp.concatenate([kept_block, flip(sent_block, group)], axis=0)

    def positions(device):
        within = jnp.arange(piece_rows, dtype=jnp.int32)
        return jnp.concatenate(
            [device * piece_rows + within, (device ^ group) * piece_rows + within]
        )

    query_pos = positions(me)
    key_pos = jnp.concatenate([positions(me ^ p) for p in range(group)])
    start = lax.dynamic_index_in_dim(image_start[:, 0], micro, 0, keepdims=False)
    query_in = (query_pos >= start) & (query_pos < start + IMG)
    key_in = (key_pos >= start) & (key_pos < start + IMG)
    allowed = (key_pos[:, None] <= query_pos[None, :]) | (key_in[:, None] & query_in[None, :])
    bias = jnp.where(allowed, 0.0, masked_value).astype(F32)
    frequency = 10000.0 ** (-jnp.arange(DH // 2, dtype=F32) / (DH // 2))
    angles = query_pos.astype(F32)[:, None] * frequency[None, :]
    cosine = jnp.tile(jnp.cos(angles), (1, 4))
    sine = jnp.sin(angles)
    sine = jnp.concatenate([-sine, sine, -sine, sine], axis=1)
    place = (group, cosine, sine, bias)

    gains = flip_gather(jnp.stack([norm_attn[0], norm_ffn[0]]), count)
    gains = put_rows(gains, [me ^ p for p in range(count)]).reshape(count, 2, -1)
    gains = gains.transpose(1, 0, 2).reshape(2, 1, -1).astype(F32)
    qkv_shard = jnp.concatenate([w_query[0], w_key[0], w_value[0]], axis=1)
    weights = (
        gather_rows(qkv_shard, count, me),
        gather_rows(w_out[0], count, me),
        gather_over_rep(w_gate[0], count, me),
        gather_over_rep(w_up[0], count, me),
        gather_rows(w_down[0], count, me),
        gains[0],
        gains[1],
    )

    _, low, _ = forward_layer(given, weights, place, "a")
    received = shifted(low, "section", 1)
    layer_in = jnp.where(is_first, given, received)
    block, _, kept = forward_layer(layer_in, weights, place, "b")
    _, low, _, _ = backward_layer(given, kept, weights, place)
    received = shifted(low, "section", -1)
    out_grad = jnp.where(is_first, received, given)
    first_grad, _, pairs, gain_grads = backward_layer(out_grad, kept, weights, place)

    lefts = {k: left_rows(v[0], me, count, group) for k, v in pairs.items()}
    rights = {k: [right_rows(right, group) for right in v[1]] for k, v in pairs.items()}
    depths = {k: v[0].shape[1] // count for k, v in pairs.items()}
    gain_sums = jnp.concatenate(gain_grads, axis=0)
    for bit in bits_below(group):
        gain_sums = gain_sums + flip(gain_sums, bit)
    gain_sums = gain_sums.reshape(2, count, depths["q"]).transpose(1, 2, 0).astype(BF16)

    def chunk(name, part, row, rows, plane, col, cols, tile_cols, gained=False):
        k = name[0]
        other, own = grad_product(
            lefts[k], rights[k][part], depths[k], row, rows, plane, col, cols, tile_cols
        )
        if gained:
            other, own = with_gains(other, me ^ group), with_gains(own, me)
        return reduced(other, own, group)

    def with_gains(product, device):
        extra = lax.dynamic_index_in_dim(gain_sums, device, 0, keepdims=False)
        return jnp.concatenate([product, jnp.pad(extra, ((0, 0), (0, KT - 2)))], axis=1)

    model = half_width * 2
    half, depth = depths["d"] // 2, depths["g"]
    wide = w_gate.shape[2] // 2
    d_grad = [chunk(f"d{i}", 0, i * half, half, 0, 0, model, model // 3) for i in range(2)]
    gu_grad = [
        chunk(f"g{i}", 0, 0, depth, i // 2, (i % 2) * wide, wide, wide // 3) for i in range(4)
    ]
    o_grad = chunk("o", 0, 0, depths["o"], 0, 0, model, WK)
    q_grad = chunk("q", 0, 0, depths["q"], 0, 0, WQ, WK)
    kv_grad = chunk("qkv", 1, 0, depths["q"], 0, 0, 2 * WK, WK, True)

    def placed(result, from_first):
        kept_rows, sent_rows = result[:piece_rows], result[piece_rows:]
        back = flip(sent_rows.astype(BF16), group).astype(F32)
        first = jnp.where(micro == 0, kept_rows, back)
        second = jnp.where(micro == 0, back, kept_rows)
        rows = jnp.stack([first, second])
        low, high = rows[..., :half_width], rows[..., half_width:]
        if from_first:
            arrived = shifted(high.astype(BF16), "section", 1)
            return jnp.where(is_first, low, arrived.astype(F32))
        arrived = shifted(low.astype(BF16), "section", -1)
        return jnp.where(is_first, arrived.astype(F32), high)

    block_out = placed(block, False)[:, None]
    input_grad = placed(first_grad, True)[:, None]
    grads = [
        q_grad,
        kv_grad[:, :WK],
        kv_grad[:, WK : 2 * WK],
        o_grad,
        jnp.concatenate(gu_grad[:2], axis=1),
        jnp.concatenate(gu_grad[2:], axis=1),
        jnp.concatenate(d_grad, axis=0),
        kv_grad[:, 2 * WK],
        kv_grad[:, 2 * WK + 1],
    ]
    return (block_out, input_grad) + tuple(grad.astype(F32)[None] for grad in grads)


def solution(mesh):
    rows = P("section", "seq", None)
    tokens = P(None, "rep", "seq", "section")
    in_specs = (tokens,) + (rows,) * 7 + (P("section", "seq"),) * 2 + (P(None, "rep"), tokens)
    out_specs = (tokens, tokens) + (rows,) * 7 + (P("section", "seq"),) * 2

    return jax.shard_map(shards, mesh=mesh, in_specs=in_specs, out_specs=out_specs, check_vma=False)
```

profile of v0, /device:TPU:0, one launch (start us, length us, event | category | flops | bytes accessed | tf_op | source)
XLA Modules:
  0.0 780.0 jit_solution(15502897929405925836)
XLA Ops:
  52.5 13.1 %collective-permute-done.19 = bf16[72,3072]{1,0:T(8,128)(2,1)S(1)} collective-permute-done((bf16[72,3072]{1,0:T(8,128)(2,1)}, bf16[72,3072]{1,0:T(8,128)(2,1)S(1)}, u32[]{:S(2)}, u32[]{:S(2)}) %collective-permute-start.19) | collective-permute-done | bytes 442400 | tf_op jit(solution)/shard_map/ppermute | solution.py:24
  90.5 11.4 %collective-permute-done.20 = bf16[72,3072]{1,0:T(8,128)(2,1)S(1)} collective-permute-done((bf16[72,3072]{1,0:T(8,128)(2,1)S(1)}, bf16[72,3072]{1,0:T(8,128)(2,1)S(1)}, u32[]{:S(2)}, u32[]{:S(2)}) %collective-permute-start.20) | collective-permute-done | bytes 442400 | tf_op jit(solution)/shard_map/ppermute | solution.py:75
  102.7 12.5 %collective-permute-done.14 = bf16[72,3072]{1,0:T(8,128)(2,1)S(1)} collective-permute-done((bf16[72,3072]{1,0:T(8,128)(2,1)S(1)}, bf16[72,3072]{1,0:T(8,128)(2,1)S(1)}, u32[]{:S(2)}, u32[]{:S(2)}) %collective-permute-start.14) | collective-permute-done | bytes 442400 | tf_op jit(solution)/shard_map/ppermute | solution.py:75
  116.0 18.5 %collective-permute-done.21 = bf16[72,3072]{1,0:T(8,128)(2,1)S(1)} collective-permute-done((bf16[72,3072]{1,0:T(8,128)(2,1)S(1)}, bf16[72,3072]{1,0:T(8,128)(2,1)S(1)}, u32[]{:S(2)}, u32[]{:S(2)}) %collective-permute-start.21) | collective-permute-done | bytes 442400 | tf_op jit(solution)/shard_map/ppermute | solution.py:75
  135.4 19.8 %collective-permute-done.15 = bf16[72,3072]{1,0:T(8,128)(2,1)S(1)} collective-permute-done((bf16[72,3072]{1,0:T(8,128)(2,1)S(1)}, bf16[72,3072]{1,0:T(8,128)(2,1)S(1)}, u32[]{:S(2)}, u32[]{:S(2)}) %collective-permute-start.15) | collective-permute-done | bytes 442400 | tf_op jit(solution)/shard_map/ppermute | solution.py:75
  207.9 11.4 %shard_map.204 = (bf16[256,1152]{1,0:T(8,128)(2,1)}, f32[3,8,256]{2,1,0:T(8,128)}) custom-call(bf16[256,1152]{1,0:T(8,128)(2,1)} %get-tuple-element.66.q_ref, bf16[512,768]{1,0:T(8,128)(2,1)} %pad_maximum_fusion.1.k_ref.v_ref, bf16[512,768]{1,0:T(8,128)(2,1)} %pad_maximum_fusion.1.k_ref.v_ref, f32[512,256]{1,0:T(8,128)} %or_select_fusion.bias_ref), custom_call_target="tpu_custom_call" | custom-call | flops 1207959552 | bytes 4194304 | tf_op jit(solution)/shard_map/pallas_call | solution.py:202
  251.6 12.8 %collective-permute-done.27 = bf16[256,1152]{1,0:T(8,128)(2,1)S(1)} collective-permute-done((bf16[256,1152]{1,0:T(8,128)(2,1)}, bf16[256,1152]{1,0:T(8,128)(2,1)S(1)}, u32[]{:S(2)}, u32[]{:S(2)}) %collective-permute-start.27) | collective-permute-done | bytes 589856 | tf_op jit(solution)/shard_map/ppermute | solution.py:30
  276.9 11.4 %shard_map.209 = (bf16[256,1152]{1,0:T(8,128)(2,1)}, f32[3,8,256]{2,1,0:T(8,128)}) custom-call(bf16[256,1152]{1,0:T(8,128)(2,1)} %get-tuple-element.72.q_ref, bf16[512,768]{1,0:T(8,128)(2,1)} %copy-done.43, bf16[512,768]{1,0:T(8,128)(2,1)} %copy-done.43, f32[512,256]{1,0:T(8,128)} %or_select_fusion.bias_ref), custom_call_target="tpu_custom_call" | custom-call | flops 1207959552 | bytes 4194304 | tf_op jit(solution)/shard_map/pallas_call | solution.py:202
  294.6 10.0 %shard_map.211 = (bf16[256,3072]{1,0:T(8,128)(2,1)}, bf16[256,3072]{1,0:T(8,128)(2,1)}, bf16[256,3072]{1,0:T(8,128)(2,1)}) custom-call(bf16[256,1152]{1,0:T(8,128)(2,1)} %get-tuple-element.75.x_ref, bf16[1152,3072]{1,0:T(8,128)(2,1)} %bitcast.34.wg_ref, bf16[1152,3072]{1,0:T(8,128)(2,1)} %bitcast.45.wu_ref), custom_call_target="tpu_custom_call" | custom-call | flops 3623878656 | bytes 18874368 | tf_op jit(solution)/shard_map/pallas_call | solution.py:337
  323.9 14.5 %shard_map.214 = (f32[256,1152]{1,0:T(8,128)}, bf16[256,1152]{1,0:T(8,128)(2,1)}, bf16[256,1152]{1,0:T(8,128)(2,1)}, f32[1,1152]{1,0:T(1,128)}) custom-call(bf16[2,256,3072]{2,1,0:T(8,128)(2,1)} %shard_map.213.d_ref, bf16[1152,3072]{1,0:T(8,128)(2,1)} %bitcast.34.wg_ref, bf16[1152,3072]{1,0:T(8,128)(2,1)} %bitcast.45.wu_ref, ...), custom_call_target="tpu_custom_call" | custom-call | flops 4303355904 | bytes 20840448 | tf_op jit(solution)/shard_map/pallas_call | solution.py:451
  338.5 13.2 %shard_map.215 = (bf16[256,1152]{1,0:T(8,128)(2,1)}, bf16[256,384]{1,0:T(8,128)(2,1)}, bf16[256,384]{1,0:T(8,128)(2,1)}, bf16[256,384]{1,0:T(8,128)(2,1)}, bf16[256,384]{1,0:T(8,128)(2,1)}) custom-call(bf16[256,1152]{1,0:T(8,128)(2,1)} %get-tuple-element.72.q_ref, bf16[512,768]{1,0:T(8,128)(2,1)} %copy-done.43, bf16[512,768]{1,0:T(8,128)(2,1)} %copy-done.43, ...), custom_call_target="tpu_custom_call" | custom-call | flops 2415919104 | bytes 8388608 | tf_op jit(solution)/shard_map/pallas_call | solution.py:265
  367.1 13.1 %collective-permute-done.33 = bf16[256,1152]{1,0:T(8,128)(2,1)S(1)} collective-permute-done((bf16[256,1152]{1,0:T(8,128)(2,1)}, bf16[256,1152]{1,0:T(8,128)(2,1)S(1)}, u32[]{:S(2)}, u32[]{:S(2)}) %collective-permute-start.33) | collective-permute-done | bytes 589856 | tf_op jit(solution)/shard_map/ppermute | solution.py:30
  388.5 14.5 %shard_map.218 = (f32[256,1152]{1,0:T(8,128)}, bf16[256,1152]{1,0:T(8,128)(2,1)}, bf16[256,1152]{1,0:T(8,128)(2,1)}, f32[1,1152]{1,0:T(1,128)}) custom-call(bf16[2,256,3072]{2,1,0:T(8,128)(2,1)} %shard_map.217.d_ref.refs_4_, bf16[1152,3072]{1,0:T(8,128)(2,1)} %bitcast.34.wg_ref, bf16[1152,3072]{1,0:T(8,128)(2,1)} %bitcast.45.wu_ref, ...), custom_call_target="tpu_custom_call" | custom-call | flops 4303355904 | bytes 20840448 | tf_op jit(solution)/shard_map/pallas_call | solution.py:451
  403.0 13.1 %shard_map.219 = (bf16[256,1152]{1,0:T(8,128)(2,1)}, bf16[256,384]{1,0:T(8,128)(2,1)}, bf16[256,384]{1,0:T(8,128)(2,1)}, bf16[256,384]{1,0:T(8,128)(2,1)}, bf16[256,384]{1,0:T(8,128)(2,1)}) custom-call(bf16[256,1152]{1,0:T(8,128)(2,1)} %get-tuple-element.72.q_ref, bf16[512,768]{1,0:T(8,128)(2,1)} %copy-done.43, bf16[512,768]{1,0:T(8,128)(2,1)} %copy-done.43, ...), custom_call_target="tpu_custom_call" | custom-call | flops 2415919104 | bytes 8388608 | tf_op jit(solution)/shard_map/pallas_call | solution.py:265
  480.1 28.2 %collective-permute-done.46 = bf16[288,896]{1,0:T(8,128)(2,1)} collective-permute-done((bf16[288,896]{1,0:T(8,128)(2,1)}, bf16[288,896]{1,0:T(8,128)(2,1)}, u32[]{:S(2)}, u32[]{:S(2)}) %collective-permute-start.46) | collective-permute-done | bytes 516128 | tf_op jit(solution)/shard_map/ppermute | solution.py:24
  516.9 10.4 %collective-permute-done.80 = bf16[384,1152]{1,0:T(8,128)(2,1)} collective-permute-done((bf16[384,1152]{1,0:T(8,128)(2,1)}, bf16[384,1152]{1,0:T(8,128)(2,1)}, u32[]{:S(2)}, u32[]{:S(2)}) %collective-permute-start.80) | collective-permute-done | bytes 884768 | tf_op jit(solution)/shard_map/ppermute | solution.py:24
  534.9 9.7 %collective-permute-done.76 = bf16[384,1152]{1,0:T(8,128)(2,1)S(1)} collective-permute-done((bf16[384,1152]{1,0:T(8,128)(2,1)}, bf16[384,1152]{1,0:T(8,128)(2,1)S(1)}, u32[]{:S(2)}, u32[]{:S(2)}) %collective-permute-start.76) | collective-permute-done | bytes 884768 | tf_op jit(solution)/shard_map/ppermute | solution.py:24
  656.1 10.6 %collective-permute-done.59 = bf16[288,1536]{1,0:T(8,128)(2,1)S(1)} collective-permute-done((bf16[288,1536]{1,0:T(8,128)(2,1)S(1)}, bf16[288,1536]{1,0:T(8,128)(2,1)S(1)}, u32[]{:S(2)}, u32[]{:S(2)}) %collective-permute-start.59) | collective-permute-done | bytes 884768 | tf_op jit(solution)/shard_map/ppermute | solution.py:89
  669.7 16.0 %collective-permute-done.71 = bf16[288,1536]{1,0:T(8,128)(2,1)S(1)} collective-permute-done((bf16[288,1536]{1,0:T(8,128)(2,1)S(1)}, bf16[288,1536]{1,0:T(8,128)(2,1)S(1)}, u32[]{:S(2)}, u32[]{:S(2)}) %collective-permute-start.71) | collective-permute-done | bytes 884768 | tf_op jit(solution)/shard_map/ppermute | solution.py:89
  686.6 12.1 %collective-permute-done.67 = bf16[288,1536]{1,0:T(8,128)(2,1)S(1)} collective-permute-done((bf16[288,1536]{1,0:T(8,128)(2,1)S(1)}, bf16[288,1536]{1,0:T(8,128)(2,1)S(1)}, u32[]{:S(2)}, u32[]{:S(2)}) %collective-permute-start.67) | collective-permute-done | bytes 884768 | tf_op jit(solution)/shard_map/ppermute | solution.py:89
  708.2 19.1 %collective-permute-done.65 = bf16[288,1536]{1,0:T(8,128)(2,1)S(1)} collective-permute-done((bf16[288,1536]{1,0:T(8,128)(2,1)S(1)}, bf16[288,1536]{1,0:T(8,128)(2,1)S(1)}, u32[]{:S(2)}, u32[]{:S(2)}) %collective-permute-start.65) | collective-permute-done | bytes 884768 | tf_op jit(solution)/shard_map/ppermute | solution.py:91
  727.5 18.9 %collective-permute-done.61 = bf16[288,1536]{1,0:T(8,128)(2,1)S(1)} collective-permute-done((bf16[288,1536]{1,0:T(8,128)(2,1)S(1)}, bf16[288,1536]{1,0:T(8,128)(2,1)S(1)}, u32[]{:S(2)}, u32[]{:S(2)}) %collective-permute-start.61) | collective-permute-done | bytes 884768 | tf_op jit(solution)/shard_map/ppermute | solution.py:91
  748.6 16.6 %collective-permute-done.73 = bf16[288,1536]{1,0:T(8,128)(2,1)S(1)} collective-permute-done((bf16[288,1536]{1,0:T(8,128)(2,1)S(1)}, bf16[288,1536]{1,0:T(8,128)(2,1)S(1)}, u32[]{:S(2)}, u32[]{:S(2)}) %collective-permute-start.73) | collective-permute-done | bytes 884768 | tf_op jit(solution)/shard_map/ppermute | solution.py:91
  765.4 11.8 %collective-permute-done.69 = bf16[288,1536]{1,0:T(8,128)(2,1)S(1)} collective-permute-done((bf16[288,1536]{1,0:T(8,128)(2,1)S(1)}, bf16[288,1536]{1,0:T(8,128)(2,1)S(1)}, u32[]{:S(2)}, u32[]{:S(2)}) %collective-permute-start.69) | collective-permute-done | bytes 884768 | tf_op jit(solution)/shard_map/ppermute | solution.py:91
  (429 shorter events, 434.0 us)
Async XLA Ops:
  7.0 173.6 %collective-permute-start.5 = (bf16[288,1920]{1,0:T(8,128)(2,1)}, bf16[288,1920]{1,0:T(8,128)(2,1)}, u32[]{:S(2)}, u32[]{:S(2)}) collective-permute-start(bf16[288,1920]{1,0:T(8,128)(2,1)} %pad_maximum_fusion), channel_id=1, source_target_pairs={{0,4},{4,0},{8,12},{12,8},{1,5},{5,1},{9,13},{13,9},{2,6},{6,2},{1... | collective-permute-start | bytes 3317768 | tf_op jit(solution)/shard_map/ppermute | solution.py:24
  7.1 176.3 %collective-permute-start.6 = (bf16[288,1920]{1,0:T(8,128)(2,1)}, bf16[288,1920]{1,0:T(8,128)(2,1)}, u32[]{:S(2)}, u32[]{:S(2)}) collective-permute-start(bf16[288,1920]{1,0:T(8,128)(2,1)} %pad_maximum_fusion), channel_id=1, source_target_pairs={{0,8},{4,12},{8,0},{12,4},{1,9},{5,13},{9,1},{13,5},{2,10},{6,14},... | collective-permute-start | bytes 3317768 | tf_op jit(solution)/shard_map/ppermute | solution.py:24
  7.4 77.7 %collective-permute-start.9 = (bf16[288,1152]{1,0:T(8,128)(2,1)}, bf16[288,1152]{1,0:T(8,128)(2,1)}, u32[]{:S(2)}, u32[]{:S(2)}) collective-permute-start(bf16[288,1152]{1,0:T(8,128)(2,1)} %bitcast.19), channel_id=1, source_target_pairs={{0,4},{4,0},{8,12},{12,8},{1,5},{5,1},{9,13},{13,9},{2,6},{6,2},{1... | collective-permute-start | bytes 1990664 | tf_op jit(solution)/shard_map/ppermute | solution.py:24
  38.9 48.9 %collective-permute-start.10 = (bf16[288,1152]{1,0:T(8,128)(2,1)}, bf16[288,1152]{1,0:T(8,128)(2,1)}, u32[]{:S(2)}, u32[]{:S(2)}) collective-permute-start(bf16[288,1152]{1,0:T(8,128)(2,1)} %bitcast.19), channel_id=1, source_target_pairs={{0,8},{4,12},{8,0},{12,4},{1,9},{5,13},{9,1},{13,5},{2,10},{6,14},... | collective-permute-start | bytes 1990664 | tf_op jit(solution)/shard_map/ppermute | solution.py:24
  84.2 106.1 %collective-permute-start.24 = (bf16[768,1152]{1,0:T(8,128)(2,1)S(1)}, bf16[768,1152]{1,0:T(8,128)(2,1)S(1)}, u32[]{:S(2)}, u32[]{:S(2)}) collective-permute-start(bf16[768,1152]{1,0:T(8,128)(2,1)S(1)} %bitcast.175), channel_id=1, source_target_pairs={{0,4},{4,0},{8,12},{12,8},{1,5},{5,1},{9,13},{13,9},{2,6},{6,2},{1... | collective-permute-start | bytes 5308424 | tf_op jit(solution)/shard_map/ppermute | solution.py:24
  85.1 103.5 %collective-permute-start.25 = (bf16[768,1152]{1,0:T(8,128)(2,1)S(1)}, bf16[768,1152]{1,0:T(8,128)(2,1)}, u32[]{:S(2)}, u32[]{:S(2)}) collective-permute-start(bf16[768,1152]{1,0:T(8,128)(2,1)S(1)} %bitcast.176), channel_id=1, source_target_pairs={{0,8},{4,12},{8,0},{12,4},{1,9},{5,13},{9,1},{13,5},{2,10},{6,14},... | collective-permute-start | bytes 5308424 | tf_op jit(solution)/shard_map/ppermute | solution.py:24
  186.4 41.0 %collective-permute-start.23 = (bf16[288,3072]{1,0:T(8,128)(2,1)}, bf16[288,3072]{1,0:T(8,128)(2,1)}, u32[]{:S(2)}, u32[]{:S(2)}) collective-permute-start(bf16[288,3072]{1,0:T(8,128)(2,1)} %bitcast.43), channel_id=1, source_target_pairs={{0,4},{4,0},{8,12},{12,8},{1,5},{5,1},{9,13},{13,9},{2,6},{6,2},{1... | collective-permute-start | bytes 5308424 | tf_op jit(solution)/shard_map/ppermute | solution.py:24
  188.6 50.5 %collective-permute-start.26 = (bf16[768,1152]{1,0:T(8,128)(2,1)}, bf16[768,1152]{1,0:T(8,128)(2,1)S(1)}, u32[]{:S(2)}, u32[]{:S(2)}) collective-permute-start(bf16[768,1152]{1,0:T(8,128)(2,1)} %collective-permute-done.25), channel_id=1, source_target_pairs={{0,4},{4,0},{8,12},{12,8},{1,5},{5,1},{9,13},{13,9},{2,6},{6,2},{1... | collective-permute-start | bytes 5308424 | tf_op jit(solution)/shard_map/ppermute | solution.py:24
  274.6 160.1 %collective-permute-start.38 = (bf16[576,256]{1,0:T(8,128)(2,1)}, bf16[576,256]{1,0:T(8,128)(2,1)S(1)}, u32[]{:S(2)}, u32[]{:S(2)}) collective-permute-start(bf16[576,256]{1,0:T(8,128)(2,1)} %pad_maximum_fusion.8), channel_id=1, source_target_pairs={{0,4},{4,0},{8,12},{12,8},{1,5},{5,1},{9,13},{13,9},{2,6},{6,2},{1... | collective-permute-start | bytes 884744 | tf_op jit(solution)/shard_map/ppermute | solution.py:24
  315.6 101.1 %collective-permute-start.29 = (bf16[128,1152]{1,0:T(8,128)(2,1)}, bf16[128,1152]{1,0:T(8,128)(2,1)}, u32[]{:S(2)}, u32[]{:S(2)}) collective-permute-start(bf16[128,1152]{1,0:T(8,128)(2,1)} %slice.107), channel_id=1, source_target_pairs={{0,8},{4,12},{8,0},{12,4},{1,9},{5,13},{9,1},{13,5},{2,10},{6,14},... | collective-permute-start | bytes 884744 | tf_op jit(solution)/shard_map/ppermute | solution.py:24
  354.1 80.8 %collective-permute-start.50 = (bf16[576,256]{1,0:T(8,128)(2,1)}, bf16[576,256]{1,0:T(8,128)(2,1)}, u32[]{:S(2)}, u32[]{:S(2)}) collective-permute-start(bf16[576,256]{1,0:T(8,128)(2,1)} %pad_maximum_fusion.10), channel_id=1, source_target_pairs={{0,4},{4,0},{8,12},{12,8},{1,5},{5,1},{9,13},{13,9},{2,6},{6,2},{1... | collective-permute-start | bytes 884744 | tf_op jit(solution)/shard_map/ppermute | solution.py:24
  429.3 124.1 %collective-permute-start.57 = (bf16[2,256,3072]{2,1,0:T(8,128)(2,1)S(1)}, bf16[2,256,3072]{2,1,0:T(8,128)(2,1)}, u32[]{:S(2)}, u32[]{:S(2)}) collective-permute-start(bf16[2,256,3072]{2,1,0:T(8,128)(2,1)S(1)} %copy-done.2), channel_id=1, source_target_pairs={{0,4},{4,0},{8,12},{12,8},{1,5},{5,1},{9,13},{13,9},{2,6},{6,2},{1... | collective-permute-start | bytes 9437192 | tf_op jit(solution)/shard_map/ppermute | solution.py:24
  464.9 45.8 %collective-permute-start.40 = (bf16[288,1152]{1,0:T(8,128)(2,1)}, bf16[288,1152]{1,0:T(8,128)(2,1)}, u32[]{:S(2)}, u32[]{:S(2)}) collective-permute-start(bf16[288,1152]{1,0:T(8,128)(2,1)} %get-tuple-element.100), channel_id=1, source_target_pairs={{0,8},{4,12},{8,0},{12,4},{1,9},{5,13},{9,1},{13,5},{2,10},{6,14},... | collective-permute-start | bytes 1990664 | tf_op jit(solution)/shard_map/ppermute | solution.py:24
  465.9 47.5 %collective-permute-start.52 = (bf16[288,1152]{1,0:T(8,128)(2,1)}, bf16[288,1152]{1,0:T(8,128)(2,1)}, u32[]{:S(2)}, u32[]{:S(2)}) collective-permute-start(bf16[288,1152]{1,0:T(8,128)(2,1)} %get-tuple-element.108), channel_id=1, source_target_pairs={{0,8},{4,12},{8,0},{12,4},{1,9},{5,13},{9,1},{13,5},{2,10},{6,14},... | collective-permute-start | bytes 1990664 | tf_op jit(solution)/shard_map/ppermute | solution.py:24
  467.0 41.3 %collective-permute-start.46 = (bf16[288,896]{1,0:T(8,128)(2,1)}, bf16[288,896]{1,0:T(8,128)(2,1)}, u32[]{:S(2)}, u32[]{:S(2)}) collective-permute-start(bf16[288,896]{1,0:T(8,128)(2,1)} %fusion.16), channel_id=1, source_target_pairs={{0,8},{4,12},{8,0},{12,4},{1,9},{5,13},{9,1},{13,5},{2,10},{6,14},... | collective-permute-start | bytes 1548296 | tf_op jit(solution)/shard_map/ppermute | solution.py:24
  474.6 52.7 %collective-permute-start.80 = (bf16[384,1152]{1,0:T(8,128)(2,1)}, bf16[384,1152]{1,0:T(8,128)(2,1)}, u32[]{:S(2)}, u32[]{:S(2)}) collective-permute-start(bf16[384,1152]{1,0:T(8,128)(2,1)} %get-tuple-element.120), channel_id=1, source_target_pairs={{0,8},{4,12},{8,0},{12,4},{1,9},{5,13},{9,1},{13,5},{2,10},{6,14},... | collective-permute-start | bytes 2654216 | tf_op jit(solution)/shard_map/ppermute | solution.py:24
  531.8 39.9 %collective-permute-start.81 = (bf16[384,1152]{1,0:T(8,128)(2,1)}, bf16[384,1152]{1,0:T(8,128)(2,1)}, u32[]{:S(2)}, u32[]{:S(2)}) collective-permute-start(bf16[384,1152]{1,0:T(8,128)(2,1)} %add.315), channel_id=1, source_target_pairs={{0,1},{3,2},{4,5},{7,6},{8,9},{11,10},{12,13},{15,14},{16,17},{19,... | collective-permute-start | bytes 2654216 | tf_op jit(solution)/shard_map/ppermute | solution.py:89
  558.9 44.5 %collective-permute-start.62 = (bf16[288,1536]{1,0:T(8,128)(2,1)}, bf16[288,1536]{1,0:T(8,128)(2,1)}, u32[]{:S(2)}, u32[]{:S(2)}) collective-permute-start(bf16[288,1536]{1,0:T(8,128)(2,1)} %get-tuple-element.112), channel_id=1, source_target_pairs={{0,8},{4,12},{8,0},{12,4},{1,9},{5,13},{9,1},{13,5},{2,10},{6,14},... | collective-permute-start | bytes 2654216 | tf_op jit(solution)/shard_map/ppermute | solution.py:24
  586.7 41.1 %collective-permute-start.82 = (bf16[384,1152]{1,0:T(8,128)(2,1)S(1)}, bf16[384,1152]{1,0:T(8,128)(2,1)}, u32[]{:S(2)}, u32[]{:S(2)}) collective-permute-start(bf16[384,1152]{1,0:T(8,128)(2,1)S(1)} %add.316), channel_id=1, source_target_pairs={{1,2},{2,1},{5,6},{6,5},{9,10},{10,9},{13,14},{14,13},{17,18},{18,... | collective-permute-start | bytes 2654216 | tf_op jit(solution)/shard_map/ppermute | solution.py:90
  645.0 56.5 %collective-permute-start.79 = (bf16[384,1152]{1,0:T(8,128)(2,1)S(1)}, bf16[384,1152]{1,0:T(8,128)(2,1)S(1)}, u32[]{:S(2)}, u32[]{:S(2)}) collective-permute-start(bf16[384,1152]{1,0:T(8,128)(2,1)S(1)} %add.314), channel_id=1, source_target_pairs={{1,0},{2,3},{5,4},{6,7},{9,8},{10,11},{13,12},{14,15},{17,16},{18,... | collective-permute-start | bytes 2654216 | tf_op jit(solution)/shard_map/ppermute | solution.py:91
  654.7 44.0 %collective-permute-start.67 = (bf16[288,1536]{1,0:T(8,128)(2,1)S(1)}, bf16[288,1536]{1,0:T(8,128)(2,1)S(1)}, u32[]{:S(2)}, u32[]{:S(2)}) collective-permute-start(bf16[288,1536]{1,0:T(8,128)(2,1)S(1)} %add.302), channel_id=1, source_target_pairs={{0,1},{3,2},{4,5},{7,6},{8,9},{11,10},{12,13},{15,14},{16,17},{19,... | collective-permute-start | bytes 2654216 | tf_op jit(solution)/shard_map/ppermute | solution.py:89
  701.8 44.5 %collective-permute-start.61 = (bf16[288,1536]{1,0:T(8,128)(2,1)S(1)}, bf16[288,1536]{1,0:T(8,128)(2,1)S(1)}, u32[]{:S(2)}, u32[]{:S(2)}) collective-permute-start(bf16[288,1536]{1,0:T(8,128)(2,1)S(1)} %add.298), channel_id=1, source_target_pairs={{1,0},{2,3},{5,4},{6,7},{9,8},{10,11},{13,12},{14,15},{17,16},{18,... | collective-permute-start | bytes 2654216 | tf_op jit(solution)/shard_map/ppermute | solution.py:91
  705.4 59.9 %collective-permute-start.73 = (bf16[288,1536]{1,0:T(8,128)(2,1)S(1)}, bf16[288,1536]{1,0:T(8,128)(2,1)S(1)}, u32[]{:S(2)}, u32[]{:S(2)}) collective-permute-start(bf16[288,1536]{1,0:T(8,128)(2,1)S(1)} %add.307), channel_id=1, source_target_pairs={{1,0},{2,3},{5,4},{6,7},{9,8},{10,11},{13,12},{14,15},{17,16},{18,... | collective-permute-start | bytes 2654216 | tf_op jit(solution)/shard_map/ppermute | solution.py:91
  706.9 70.3 %collective-permute-start.69 = (bf16[288,1536]{1,0:T(8,128)(2,1)S(1)}, bf16[288,1536]{1,0:T(8,128)(2,1)S(1)}, u32[]{:S(2)}, u32[]{:S(2)}) collective-permute-start(bf16[288,1536]{1,0:T(8,128)(2,1)S(1)} %add.304), channel_id=1, source_target_pairs={{1,0},{2,3},{5,4},{6,7},{9,8},{10,11},{13,12},{14,15},{17,16},{18,... | collective-permute-start | bytes 2654216 | tf_op jit(solution)/shard_map/ppermute | solution.py:91
  (114 other events, 1662.2 us)
where the time goes:
time: 789 us; the launch traced here: 780 us
  waiting for transfers between devices  314 us (40%)
  Pallas kernels  200 us (25%)
  starting transfers between devices  102 us (13%)
  local copies, waits for them, and re-layouts  84.1 us (11%)
  other arithmetic  76.4 us (10%)
    ppermute x47, waiting for transfers between devices, flip(): lax.ppermute(block, axis, [(i, i ^ bit) for i in range(lax.axis_size(axis...  89.1 us
    ppermute x6, waiting for transfers between devices, gather_over_rep(): lax.ppermute(part, 'rep', [(i, (i + k) % reps) for i in range(reps)])  78.5 us
    ppermute x9, waiting for transfers between devices, rep_sum(): arrived = lax.ppermute(value, 'rep', [(1, 0), (2, 3)])  66.5 us
    ppermute x9, waiting for transfers between devices, rep_sum(): value = value + lax.ppermute(value, 'rep', [(0, 1), (3, 2)])  54.5 us
    dynamic_update_slice x30, local copies, waits for them, and re-layouts, put_rows(): lax.dynamic_update_slice(whole, piece[None], (place,) + (0,) * piece.ndim)  38.1 us
    pallas_call x9, Pallas kernels, grad_product(): kernel(grad_kernel, 4 * total * tokens * rows * cols, 8 * rows * cols, gr...  36.5 us
    ppermute x9, starting transfers between devices, rep_sum(): value = value + lax.ppermute(value, 'rep', [(0, 1), (3, 2)])  29.9 us
    ppermute x47, starting transfers between devices, flip(): lax.ppermute(block, axis, [(i, i ^ bit) for i in range(lax.axis_size(axis...  29.1 us
  transfers between devices with their start and end apart: 84, of which 27 were waited for; matrix products, arithmetic and copies ran while one was open for 19% of the time, Pallas kernels for 24%

commit v1 on v0

--- a/solution.py
+++ b/solution.py
@@ -1,3 +1,5 @@
+import functools
+
 import jax
 import jax.numpy as jnp
 from jax import lax
@@ -52,32 +54,66 @@
         held = {p: held[p] + added[p] for p in kept}
 
 
-def put_rows(pieces, places):
-    whole = jnp.zeros((len(pieces),) + pieces[0].shape, pieces[0].dtype)
-    for place, piece in zip(places, pieces):
-        whole = lax.dynamic_update_slice(whole, piece[None], (place,) + (0,) * piece.ndim)
-    return whole.reshape((len(pieces) * pieces[0].shape[0],) + pieces[0].shape[1:])
-
-
-def gather_rows(shard, count, me):
-    pieces = flip_gather(shard, count)
-    return put_rows(pieces, [me ^ p for p in range(count)])
-
-
-def gather_over_rep(shard, count, me):
+def row_pieces(shard, count):
+    return {"pieces": flip_gather(shard, count), "parts": None}
+
+
+def column_pieces(shard, count):
     reps = lax.axis_size("rep")
-    if count != 4 or shard.shape[0] % (8 * reps):
-        return gather_rows(shard, count, me)
+    if count != 4 or reps != 4:
+        return row_pieces(shard, count)
     here = lax.axis_index("rep")
-    depth = shard.shape[0] // reps
-    part = flip(lax.dynamic_slice_in_dim(shard, here * depth, depth, 0), 2)
+    width = shard.shape[1] // reps
+    part = flip(lax.dynamic_slice_in_dim(shard, here * width, width, 1), 2)
     parts = [part] + [
         lax.ppermute(part, "rep", [(i, (i + k) % reps) for i in range(reps)])
         for k in range(1, reps)
     ]
-    across = put_rows(parts, [(here - k) % reps for k in range(reps)])
-    pieces = [shard, flip(shard, 1), across, flip(across, 1)]
-    return put_rows(pieces, [me ^ p for p in range(count)])
+    across = [flip(piece, 1) for piece in parts]
+    return {"pieces": [shard, flip(shard, 1)], "parts": (parts, across)}
+
+
+def arrays_of(weight):
+    if weight["parts"] is None:
+        return weight["pieces"]
+    return weight["pieces"] + weight["parts"][0] + weight["parts"][1]
+
+
+def copies_of(weight, refs, ids_ref, tile, width, target, sems):
+    pieces = len(weight["pieces"])
+    depth = weight["pieces"][0].shape[0]
+    me = ids_ref[0]
+    column = tile_column(weight, ids_ref, tile) * width
+    if not isinstance(column, int):
+        column = pl.multiple_of(column, width)
+
+    def rows(p):
+        return pl.ds(pl.multiple_of((me ^ p) * depth, depth), depth)
+
+    copies = [
+        pltpu.make_async_copy(
+            refs[p].at[:, pl.ds(column, width)], target.at[rows(p), :], sems.at[p]
+        )
+        for p in range(pieces)
+    ]
+    if weight["parts"] is not None:
+        total = len(weight["parts"][0])
+        for p in (2, 3):
+            ref = refs[pieces + (p - 2) * total + tile]
+            copies.append(pltpu.make_async_copy(ref, target.at[rows(p), :], sems.at[p]))
+    return copies
+
+
+def tile_column(weight, ids_ref, tile):
+    if weight["parts"] is None:
+        return tile
+    total = len(weight["parts"][0])
+    return lax.rem(ids_ref[1] + (total - tile), total)
+
+
+def when_step(steps, body):
+    for step in range(steps):
+        pl.when(pl.program_id(0) == step)(functools.partial(body, step))
 
 
 def rep_sum(value):
@@ -86,12 +122,24 @@
         return lax.psum(value, "rep").astype(BF16)
     here = lax.axis_index("rep")
     inner = (here == 1) | (here == 2)
-    value = value + lax.ppermute(value, "rep", [(0, 1), (3, 2)])
-    value = value + lax.ppermute(value, "rep", [(1, 2), (2, 1)])
+    arrived = lax.ppermute(value, "rep", [(0, 1), (3, 2)])
+    value = plus(value, arrived)
+    arrived = lax.ppermute(value, "rep", [(1, 2), (2, 1)])
+    value = plus(value, arrived)
     arrived = lax.ppermute(value, "rep", [(1, 0), (2, 3)])
     return jnp.where(inner, value, arrived)
 
 
+def plus(left, right):
+    def body(left_ref, right_ref, out_ref):
+        out_ref[...] = left_ref[...] + right_ref[...]
+
+    rows, cols = left.shape
+    return kernel(
+        body, left.size, 6 * left.size, vmem=4, out_shape=shape_of(rows, cols)
+    )(left, right)
+
+
 def dot_nn(left, right):
     return jnp.dot(left, right, preferred_element_type=F32)
 
@@ -104,13 +152,22 @@
     return lax.rsqrt(jnp.mean(hidden * hidden, axis=-1, keepdims=True) + 1e-05)
 
 
-def kernel(body, flops, size, **options):
+def kernel(body, flops, size, scalars=0, vmem=12, **options):
     cost = pl.CostEstimate(flops=flops, bytes_accessed=size, transcendentals=0)
-    return pl.pallas_call(body, cost_estimate=cost, **options)
+    if scalars:
+        fields = ("grid", "in_specs", "out_specs", "scratch_shapes")
+        options["grid_spec"] = pltpu.PrefetchScalarGridSpec(
+            num_scalar_prefetch=scalars, **{k: options.pop(k) for k in fields if k in options}
+        )
+    params = pltpu.CompilerParams(vmem_limit_bytes=vmem << 20)
+    return pl.pallas_call(body, cost_estimate=cost, compiler_params=params, **options)
 
 
 def shape_of(rows, cols, kind=BF16):
     return jax.ShapeDtypeStruct((rows, cols), kind)
+
+
+ANY = pl.BlockSpec(memory_space=pl.ANY)
 
 
 def fixed(*extent):
@@ -123,56 +180,70 @@
     return jnp.where(low, pltpu.roll(tile, KT - DH // 2, 1), pltpu.roll(tile, DH // 2, 1))
 
 
-def project_kernel(h_ref, gain_ref, w_ref, cos_ref, sin_ref, normed_ref, q_ref, kv_ref):
-    step = pl.program_id(0)
-
-    @pl.when(step == 0)
-    def _():
-        hidden = h_ref[...].astype(F32)
-        normed_ref[...] = (hidden * inverse_rms(hidden) * gain_ref[...]).astype(BF16)
-
-    product = dot_nn(normed_ref[...], w_ref[...])
-
-    def turned(scale, out_ref):
-        for start in range(0, WK, KT):
-            tile = product[:, start : start + KT]
-            result = tile * cos_ref[...] + other_half(tile) * sin_ref[...]
-            out_ref[:, start : start + KT] = (result * scale).astype(BF16)
-
-    @pl.when(step < GROUP)
-    def _():
-        turned(DH ** (-0.5), q_ref)
-
-    @pl.when(step == GROUP)
-    def _():
-        turned(1.0, kv_ref)
-
-    @pl.when(step == GROUP + 1)
-    def _():
-        kv_ref[...] = product.astype(BF16)
-
-
-def project(hidden, gain, w_qkv, cosine, sine):
+def project(ids, hidden, gain, w_qkv, cosine, sine):
     rows, model = hidden.shape
-    return kernel(
-        project_kernel,
-        2 * rows * w_qkv.size,
-        2 * w_qkv.size + 8 * hidden.size,
-        grid=(GROUP + 2,),
-        in_specs=[
-            fixed(rows, model),
-            fixed(1, model),
-            pl.BlockSpec((model, WK), lambda j: (0, j)),
-            fixed(rows, KT),
-            fixed(rows, KT),
-        ],
+    arrays = arrays_of(w_qkv)
+    steps = GROUP + 2
+
+    def body(ids_ref, h_ref, gain_ref, cos_ref, sin_ref, *rest):
+        w_refs, (normed_ref, q_ref, kv_ref, buffer, sems) = rest[: len(arrays)], rest[len(arrays) :]
+        step = pl.program_id(0)
+        batches = [
+            copies_of(w_qkv, w_refs, ids_ref, k, WK, buffer.at[k], sems.at[k]) for k in range(steps)
+        ]
+
+        @pl.when(step == 0)
+        def _():
+            for batch in batches:
+                for copy in batch:
+                    copy.start()
+            hidden = h_ref[...].astype(F32)
+            normed_ref[...] = (hidden * inverse_rms(hidden) * gain_ref[...]).astype(BF16)
+
+        def wait(k):
+            for copy in batches[k]:
+                copy.wait()
+
+        when_step(steps, wait)
+        product = dot_nn(normed_ref[...], buffer[step])
+
+        def turned(scale, out_ref):
+            for start in range(0, WK, KT):
+                tile = product[:, start : start + KT]
+                result = tile * cos_ref[...] + other_half(tile) * sin_ref[...]
+                out_ref[:, start : start + KT] = (result * scale).astype(BF16)
+
+        @pl.when(step < GROUP)
+        def _():
+            turned(DH ** (-0.5), q_ref)
+
+        @pl.when(step == GROUP)
+        def _():
+            turned(1.0, kv_ref)
+
+        @pl.when(step == GROUP + 1)
+        def _():
+            kv_ref[...] = product.astype(BF16)
+
+    return kernel(
+        body,
+        2 * rows * model * steps * WK,
+        2 * model * steps * WK + 8 * hidden.size,
+        scalars=1,
+        grid=(steps,),
+        in_specs=[fixed(rows, model), fixed(1, model), fixed(rows, KT), fixed(rows, KT)]
+        + [ANY] * len(arrays),
         out_specs=[
             fixed(rows, model),
-            pl.BlockSpec((rows, WK), lambda j: (0, jnp.minimum(j, GROUP - 1))),
-            pl.BlockSpec((rows, WK), lambda j: (0, jnp.maximum(j - GROUP, 0))),
+            pl.BlockSpec((rows, WK), lambda j, ids: (0, jnp.minimum(j, GROUP - 1))),
+            pl.BlockSpec((rows, WK), lambda j, ids: (0, jnp.maximum(j - GROUP, 0))),
         ],
         out_shape=(shape_of(rows, model), shape_of(rows, WQ), shape_of(rows, 2 * WK)),
-    )(hidden, gain, w_qkv, cosine, sine)
+        scratch_shapes=[
+            pltpu.VMEM((steps, model, WK), BF16),
+            pltpu.SemaphoreType.DMA((steps, len(arrays))),
+        ],
+    )(ids, hidden, gain, cosine, sine, *arrays)
 
 
 def attend_kernel(q_ref, k_ref, v_ref, bias_ref, o_ref, lse_ref):
@@ -282,127 +353,189 @@
     )(queries, keys_values, keys_values, d_mixed, bias, lse, cosine, sine)
 
 
-def mix_kernel(mixed_ref, w_ref, h_ref, gain_ref, middle_ref, ffn_ref):
-    step = pl.program_id(0)
-
-    @pl.when(step == 0)
-    def _():
-        middle_ref[...] = h_ref[...].astype(F32)
-
-    middle_ref[...] += dot_nn(mixed_ref[...], w_ref[...])
-
-    @pl.when(step == pl.num_programs(0) - 1)
-    def _():
+def mix(ids, mixed, w_out, hidden, gain):
+    rows, model = hidden.shape
+    arrays = arrays_of(w_out)
+    steps = model // WK
+
+    def body(ids_ref, mixed_ref, h_ref, gain_ref, *rest):
+        w_refs, (middle_ref, ffn_ref, buffer, sems) = rest[: len(arrays)], rest[len(arrays) :]
+        batches = [
+            copies_of(w_out, w_refs, ids_ref, k, WK, buffer.at[k], sems.at[k]) for k in range(steps)
+        ]
+        for batch in batches:
+            for copy in batch:
+                copy.start()
+        for k in range(steps):
+            for copy in batches[k]:
+                copy.wait()
+            span = slice(k * WK, (k + 1) * WK)
+            product = dot_nn(mixed_ref[...], buffer[k])
+            middle_ref[:, span] = h_ref[:, span].astype(F32) + product
         middle = middle_ref[...]
         ffn_ref[...] = (middle * inverse_rms(middle) * gain_ref[...]).astype(BF16)
 
-
-def mix(mixed, w_out, hidden, gain):
-    rows, model = hidden.shape
-    tile = WK
-    return kernel(
-        mix_kernel,
-        2 * rows * w_out.size,
-        2 * w_out.size + 8 * hidden.size,
-        grid=(WQ // tile,),
-        in_specs=[
-            pl.BlockSpec((rows, tile), lambda j: (0, j)),
-            pl.BlockSpec((tile, model), lambda j: (j, 0)),
-            fixed(rows, model),
-            fixed(1, model),
-        ],
+    return kernel(
+        body,
+        2 * rows * WQ * model,
+        2 * WQ * model + 8 * hidden.size,
+        scalars=1,
+        grid=(1,),
+        in_specs=[fixed(rows, WQ), fixed(rows, model), fixed(1, model)] + [ANY] * len(arrays),
         out_specs=[fixed(rows, model), fixed(rows, model)],
         out_shape=(shape_of(rows, model, F32), shape_of(rows, model)),
-    )(mixed, w_out, hidden, gain)
-
-
-def gate_kernel(x_ref, wg_ref, wu_ref, inner_ref, *slope_refs):
-    gate = dot_nn(x_ref[...], wg_ref[...])
-    up = dot_nn(x_ref[...], wu_ref[...])
-    sig = 1.0 / (1.0 + jnp.exp(-gate))
-    silu = gate * sig
-    inner_ref[...] = (silu * up).astype(BF16)
-    if slope_refs:
-        slope_refs[0][...] = (up * (sig * (1.0 + gate * (1.0 - sig)))).astype(BF16)
-        slope_refs[1][...] = silu.astype(BF16)
-
-
-def gate_up(ffn_in, w_gate, w_up, slopes):
+        scratch_shapes=[
+            pltpu.VMEM((steps, WQ, WK), BF16),
+            pltpu.SemaphoreType.DMA((steps, len(arrays))),
+        ],
+    )(ids, mixed, hidden, gain, *arrays)
+
+
+FF_TILES = 4
+
+
+def gate_up(ids, ffn_in, w_gate, w_up, slopes):
     rows, model = ffn_in.shape
-    width = w_gate.shape[1]
-    tile = width // 4
+    width = w_gate["pieces"][0].shape[1]
+    tile = width // FF_TILES
+    arrays = arrays_of(w_gate)
+    total = len(arrays)
     outs = 3 if slopes else 1
-    cols = pl.BlockSpec((rows, tile), lambda j: (0, j))
-    weight = pl.BlockSpec((model, tile), lambda j: (0, j))
-    return kernel(
-        gate_kernel,
-        4 * rows * w_gate.size,
-        4 * w_gate.size + 2 * outs * rows * width,
-        grid=(width // tile,),
-        in_specs=[fixed(rows, model), weight, weight],
+
+    def body(ids_ref, x_ref, *rest):
+        refs = (rest[:total], rest[total : 2 * total])
+        out_refs = rest[2 * total : 2 * total + outs]
+        buffer, sems = rest[2 * total + outs :]
+        step = pl.program_id(0)
+        batches = [
+            [
+                copy
+                for i, weight in enumerate((w_gate, w_up))
+                for copy in copies_of(
+                    weight, refs[i], ids_ref, k, tile, buffer.at[k, i], sems.at[k, i]
+                )
+            ]
+            for k in range(FF_TILES)
+        ]
+
+        @pl.when(step == 0)
+        def _():
+            for batch in batches:
+                for copy in batch:
+                    copy.start()
+
+        def wait(k):
+            for copy in batches[k]:
+                copy.wait()
+
+        when_step(FF_TILES, wait)
+        gate = dot_nn(x_ref[...], buffer[step, 0])
+        up = dot_nn(x_ref[...], buffer[step, 1])
+        sig = 1.0 / (1.0 + jnp.exp(-gate))
+        silu = gate * sig
+        out_refs[0][...] = (silu * up).astype(BF16)
+        if slopes:
+            out_refs[1][...] = (up * (sig * (1.0 + gate * (1.0 - sig)))).astype(BF16)
+            out_refs[2][...] = silu.astype(BF16)
+
+    cols = pl.BlockSpec((rows, tile), lambda j, ids: (0, tile_column(w_gate, ids, j)))
+    return kernel(
+        body,
+        4 * rows * model * width,
+        4 * model * width + 2 * outs * rows * width,
+        scalars=1,
+        vmem=24,
+        grid=(FF_TILES,),
+        in_specs=[fixed(rows, model)] + [ANY] * (2 * total),
         out_specs=[cols] * outs,
         out_shape=(shape_of(rows, width),) * outs,
-    )(ffn_in, w_gate, w_up)
-
-
-def down_kernel(inner_ref, w_ref, middle_ref, out_ref, low_ref):
-    step = pl.program_id(0)
-
-    @pl.when(step == 0)
-    def _():
-        out_ref[...] = middle_ref[...]
-
-    out_ref[...] += dot_nn(inner_ref[...], w_ref[...])
-
-    @pl.when(step == pl.num_programs(0) - 1)
-    def _():
-        low_ref[...] = out_ref[...].astype(BF16)
-
-
-def down(inner, w_down, middle):
+        scratch_shapes=[
+            pltpu.VMEM((FF_TILES, 2, model, tile), BF16),
+            pltpu.SemaphoreType.DMA((FF_TILES, 2, total)),
+        ],
+    )(ids, ffn_in, *arrays, *arrays_of(w_up))
+
+
+def piece_block(rows, depth):
+    return pl.BlockSpec((rows, depth), lambda j, ids: (0, ids[0] ^ j))
+
+
+def down(ids, inner, w_down, middle):
     rows, model = middle.shape
-    width = w_down.shape[0]
-    tile = width // 4
-    return kernel(
-        down_kernel,
-        2 * rows * w_down.size,
-        2 * w_down.size + 12 * middle.size,
-        grid=(width // tile,),
-        in_specs=[
-            pl.BlockSpec((rows, tile), lambda j: (0, j)),
-            pl.BlockSpec((tile, model), lambda j: (j, 0)),
-            fixed(rows, model),
-        ],
+    pieces = w_down["pieces"]
+    total, depth = len(pieces), pieces[0].shape[0]
+
+    def body(ids_ref, inner_ref, middle_ref, *rest):
+        w_refs, (out_ref, low_ref, buffer, sems) = rest[:total], rest[total:]
+        step = pl.program_id(0)
+        copies = [pltpu.make_async_copy(w_refs[k], buffer.at[k], sems.at[k]) for k in range(total)]
+
+        @pl.when(step == 0)
+        def _():
+            for copy in copies:
+                copy.start()
+            out_ref[...] = middle_ref[...]
+
+        when_step(total, lambda k: copies[k].wait())
+        out_ref[...] += dot_nn(inner_ref[...], buffer[step])
+
+        @pl.when(step == total - 1)
+        def _():
+            low_ref[...] = out_ref[...].astype(BF16)
+
+    return kernel(
+        body,
+        2 * rows * model * depth * total,
+        2 * model * depth * total + 12 * middle.size,
+        scalars=1,
+        vmem=20,
+        grid=(total,),
+        in_specs=[piece_block(rows, depth), fixed(rows, model)] + [ANY] * total,
         out_specs=[fixed(rows, model), fixed(rows, model)],
         out_shape=(shape_of(rows, model, F32), shape_of(rows, model)),
-    )(inner, w_down, middle)
-
-
-def d_inner_kernel(g_ref, w_ref, gate_slope_ref, up_slope_ref, out_ref):
-    d_inner = dot_nt(g_ref[...], w_ref[...])
-    out_ref[0] = (d_inner * gate_slope_ref[...].astype(F32)).astype(BF16)
-    out_ref[1] = (d_inner * up_slope_ref[...].astype(F32)).astype(BF16)
-
-
-def d_inner(grad, w_down, gate_slope, up_slope):
+        scratch_shapes=[
+            pltpu.VMEM((total, depth, model), BF16),
+            pltpu.SemaphoreType.DMA((total,)),
+        ],
+    )(ids, inner, middle, *pieces)
+
+
+def d_inner(ids, grad, w_down, gate_slope, up_slope):
     rows, model = grad.shape
-    width = w_down.shape[0]
-    tile = width // 4
-    cols = pl.BlockSpec((rows, tile), lambda j: (0, j))
-    return kernel(
-        d_inner_kernel,
-        2 * rows * w_down.size,
-        2 * w_down.size + 8 * rows * width,
-        grid=(width // tile,),
-        in_specs=[
-            fixed(rows, model),
-            pl.BlockSpec((tile, model), lambda j: (j, 0)),
-            cols,
-            cols,
-        ],
-        out_specs=pl.BlockSpec((2, rows, tile), lambda j: (0, 0, j)),
-        out_shape=jax.ShapeDtypeStruct((2, rows, width), BF16),
-    )(grad, w_down, gate_slope, up_slope)
+    pieces = w_down["pieces"]
+    total, depth = len(pieces), pieces[0].shape[0]
+
+    def body(ids_ref, g_ref, gate_slope_ref, up_slope_ref, *rest):
+        w_refs, (out_ref, buffer, sems) = rest[:total], rest[total:]
+        step = pl.program_id(0)
+        copies = [pltpu.make_async_copy(w_refs[k], buffer.at[k], sems.at[k]) for k in range(total)]
+
+        @pl.when(step == 0)
+        def _():
+            for copy in copies:
+                copy.start()
+
+        when_step(total, lambda k: copies[k].wait())
+        product = dot_nt(g_ref[...], buffer[step])
+        out_ref[0] = (product * gate_slope_ref[...].astype(F32)).astype(BF16)
+        out_ref[1] = (product * up_slope_ref[...].astype(F32)).astype(BF16)
+
+    return kernel(
+        body,
+        2 * rows * model * depth * total,
+        2 * model * depth * total + 8 * rows * depth * total,
+        scalars=1,
+        vmem=20,
+        grid=(total,),
+        in_specs=[fixed(rows, model), piece_block(rows, depth), piece_block(rows, depth)]
+        + [ANY] * total,
+        out_specs=pl.BlockSpec((2, rows, depth), lambda j, ids: (0, 0, ids[0] ^ j)),
+        out_shape=jax.ShapeDtypeStruct((2, rows, depth * total), BF16),
+        scratch_shapes=[
+            pltpu.VMEM((total, depth, model), BF16),
+            pltpu.SemaphoreType.DMA((total,)),
+        ],
+    )(ids, grad, gate_slope, up_slope, *pieces)
 
 
 def norm_back(hidden, gain, d_normed):
@@ -413,55 +546,74 @@
     return back, jnp.sum(d_normed * hidden * inverse, axis=0, keepdims=True)
 
 
-def d_middle_kernel(
-    d_ref, wg_ref, wu_ref, middle_ref, gain_ref, g_ref, wo_ref,
-    dm_ref, low_ref, mixed_ref, gain_grad_ref, total,
-):
-    step = pl.program_id(0)
-    half = pl.num_programs(0) // 2
-
-    @pl.when(step == 0)
-    def _():
-        total[...] = jnp.zeros_like(total)
-
-    @pl.when(step < half)
-    def _():
-        total[...] += dot_nt(d_ref[0], wg_ref[...])
-
-    @pl.when(step >= half)
-    def _():
-        total[...] += dot_nt(d_ref[0], wu_ref[...])
-
-    @pl.when(step == pl.num_programs(0) - 1)
-    def _():
-        back, gain_grad = norm_back(middle_ref[...], gain_ref[...], total[...])
-        d_middle = g_ref[...].astype(F32) + back
-        dm_ref[...] = d_middle
-        low = d_middle.astype(BF16)
-        low_ref[...] = low
-        mixed_ref[...] = dot_nt(low, wo_ref[...]).astype(BF16)
-        gain_grad_ref[...] = gain_grad
-
-
-def d_middle(d_gu, w_gate, w_up, middle, gain, grad, w_out):
+def d_middle(ids, d_gu, w_gate, w_up, middle, gain, grad, w_out):
     rows, model = middle.shape
-    width = w_gate.shape[1]
-    tile = width // 2
-    half = width // tile
-    return kernel(
-        d_middle_kernel,
-        4 * rows * w_gate.size + 2 * rows * w_out.size,
-        4 * w_gate.size + 4 * rows * width + 12 * middle.size,
-        grid=(2 * half,),
-        in_specs=[
-            pl.BlockSpec((1, rows, tile), lambda j: (j // half, 0, j % half)),
-            pl.BlockSpec((model, tile), lambda j: (0, jnp.minimum(j, half - 1))),
-            pl.BlockSpec((model, tile), lambda j: (0, jnp.maximum(j - half, 0))),
-            fixed(rows, model),
-            fixed(1, model),
-            fixed(rows, model),
-            fixed(*w_out.shape),
-        ],
+    width = w_gate["pieces"][0].shape[1]
+    tile = width // FF_TILES
+    arrays, out_arrays = arrays_of(w_gate), arrays_of(w_out)
+    total, out_total = len(arrays), len(out_arrays)
+
+    def body(ids_ref, d_ref, middle_ref, gain_ref, g_ref, *rest):
+        refs = (rest[:total], rest[total : 2 * total])
+        out_refs = rest[2 * total : 2 * total + out_total]
+        dm_ref, low_ref, mixed_ref, gain_grad_ref, sum_ref, buffer, sems, last, last_sems = rest[
+            2 * total + out_total :
+        ]
+        step = pl.program_id(0)
+        batches = [
+            [
+                copy
+                for i, weight in enumerate((w_gate, w_up))
+                for copy in copies_of(
+                    weight, refs[i], ids_ref, k, tile, buffer.at[k, i], sems.at[k, i]
+                )
+            ]
+            for k in range(FF_TILES)
+        ]
+        last_copies = copies_of(w_out, out_refs, ids_ref, 0, model, last, last_sems)
+
+        @pl.when(step == 0)
+        def _():
+            for batch in batches + [last_copies]:
+                for copy in batch:
+                    copy.start()
+
+        def wait(k):
+            for copy in batches[k]:
+                copy.wait()
+
+        when_step(FF_TILES, wait)
+        term = dot_nt(d_ref[0], buffer[step, 0]) + dot_nt(d_ref[1], buffer[step, 1])
+
+        @pl.when(step == 0)
+        def _():
+            sum_ref[...] = term
+
+        @pl.when(step > 0)
+        def _():
+            sum_ref[...] += term
+
+        @pl.when(step == FF_TILES - 1)
+        def _():
+            back, gain_grad = norm_back(middle_ref[...], gain_ref[...], sum_ref[...])
+            d_middle = g_ref[...].astype(F32) + back
+            dm_ref[...] = d_middle
+            low_ref[...] = d_middle.astype(BF16)
+            gain_grad_ref[...] = gain_grad
+            for copy in last_copies:
+                copy.wait()
+            mixed_ref[...] = dot_nt(low_ref[...], last[...]).astype(BF16)
+
+    columns = pl.BlockSpec((2, rows, tile), lambda j, ids: (0, 0, tile_column(w_gate, ids, j)))
+    return kernel(
+        body,
+        4 * rows * model * width + 2 * rows * model * WQ,
+        4 * model * width + 4 * rows * width + 12 * middle.size,
+        scalars=1,
+        vmem=32,
+        grid=(FF_TILES,),
+        in_specs=[columns, fixed(rows, model), fixed(1, model), fixed(rows, model)]
+        + [ANY] * (2 * total + out_total),
         out_specs=[fixed(rows, model)] * 2 + [fixed(rows, WQ), fixed(1, model)],
         out_shape=(
             shape_of(rows, model, F32),
@@ -469,68 +621,106 @@
             shape_of(rows, WQ),
             shape_of(1, model, F32),
         ),
-        scratch_shapes=[pltpu.VMEM((rows, model), F32)],
-    )(d_gu, w_gate, w_up, middle, gain, grad, w_out)
-
-
-def d_hidden_kernel(
-    dq_ref, dk_ref, dv_ref, dk2_ref, dv2_ref, cos_ref, sin_ref, w_ref, h_ref, gain_ref, dm_ref,
-    dkv_ref, dh_ref, low_ref, gain_grad_ref,
-):
-    for start in range(0, WK, KT):
-        tile = dk_ref[:, start : start + KT].astype(F32)
-        tile += dk2_ref[:, start : start + KT].astype(F32)
-        turned = tile * cos_ref[...] - other_half(tile) * sin_ref[...]
-        dkv_ref[:, start : start + KT] = turned.astype(BF16)
-    dkv_ref[:, WK:] = (dv_ref[...].astype(F32) + dv2_ref[...].astype(F32)).astype(BF16)
-    d_normed = dot_nt(dq_ref[...], w_ref[:, :WQ]) + dot_nt(dkv_ref[...], w_ref[:, WQ:])
-    back, gain_grad = norm_back(h_ref[...].astype(F32), gain_ref[...], d_normed)
-    d_hidden = dm_ref[...] + back
-    dh_ref[...] = d_hidden
-    low_ref[...] = d_hidden.astype(BF16)
-    gain_grad_ref[...] = gain_grad
-
-
-def d_hidden(dq, dkv, cosine, sine, w_qkv, hidden, gain, d_mid):
+        scratch_shapes=[
+            pltpu.VMEM((rows, model), F32),
+            pltpu.VMEM((FF_TILES, 2, model, tile), BF16),
+            pltpu.SemaphoreType.DMA((FF_TILES, 2, total)),
+            pltpu.VMEM((WQ, model), BF16),
+            pltpu.SemaphoreType.DMA((out_total,)),
+        ],
+    )(ids, d_gu, middle, gain, grad, *arrays, *arrays_of(w_up), *out_arrays)
+
+
+def d_hidden(ids, dq, dkv, cosine, sine, w_qkv, hidden, gain, d_mid):
     rows, model = hidden.shape
-    return kernel(
-        d_hidden_kernel,
-        2 * rows * w_qkv.size,
-        2 * w_qkv.size + 16 * hidden.size,
+    arrays = arrays_of(w_qkv)
+    steps = GROUP + 2
+
+    def body(
+        ids_ref, dq_ref, dk_ref, dv_ref, dk2_ref, dv2_ref, cos_ref, sin_ref, h_ref, gain_ref,
+        dm_ref, *rest,
+    ):
+        w_refs = rest[: len(arrays)]
+        dkv_ref, dh_ref, low_ref, gain_grad_ref, buffer, sems = rest[len(arrays) :]
+        batches = [
+            copies_of(w_qkv, w_refs, ids_ref, k, WK, buffer.at[k], sems.at[k]) for k in range(steps)
+        ]
+        for batch in batches:
+            for copy in batch:
+                copy.start()
+        for start in range(0, WK, KT):
+            tile = dk_ref[:, start : start + KT].astype(F32)
+            tile += dk2_ref[:, start : start + KT].astype(F32)
+            turned = tile * cos_ref[...] - other_half(tile) * sin_ref[...]
+            dkv_ref[:, start : start + KT] = turned.astype(BF16)
+        dkv_ref[:, WK:] = (dv_ref[...].astype(F32) + dv2_ref[...].astype(F32)).astype(BF16)
+        d_normed = None
+        for k in range(steps):
+            for copy in batches[k]:
+                copy.wait()
+            if k < GROUP:
+                operand = dq_ref[:, k * WK : (k + 1) * WK]
+            else:
+                operand = dkv_ref[:, (k - GROUP) * WK : (k - GROUP + 1) * WK]
+            term = dot_nt(operand, buffer[k])
+            d_normed = term if d_normed is None else d_normed + term
+        back, gain_grad = norm_back(h_ref[...].astype(F32), gain_ref[...], d_normed)
+        d_hidden = dm_ref[...] + back
+        dh_ref[...] = d_hidden
+        low_ref[...] = d_hidden.astype(BF16)
+        gain_grad_ref[...] = gain_grad
+
+    narrow = fixed(rows, WK)
+    return kernel(
+        body,
+        2 * rows * model * steps * WK,
+        2 * model * steps * WK + 16 * hidden.size,
+        scalars=1,
+        grid=(1,),
+        in_specs=[fixed(rows, WQ)]
+        + [narrow] * 4
+        + [fixed(rows, KT)] * 2
+        + [fixed(rows, model), fixed(1, model), fixed(rows, model)]
+        + [ANY] * len(arrays),
+        out_specs=[fixed(rows, 2 * WK), fixed(rows, model), fixed(rows, model), fixed(1, model)],
         out_shape=(
             shape_of(rows, 2 * WK),
             shape_of(rows, model, F32),
             shape_of(rows, model),
             shape_of(1, model, F32),
         ),
-    )(dq, *dkv, cosine, sine, w_qkv, hidden, gain, d_mid)
+        scratch_shapes=[
+            pltpu.VMEM((steps, model, WK), BF16),
+            pltpu.SemaphoreType.DMA((steps, len(arrays))),
+        ],
+    )(ids, dq, *dkv, cosine, sine, hidden, gain, d_mid, *arrays)
 
 
 def forward_layer(hidden, weights, place, tick):
     w_qkv, w_out, w_gate, w_up, w_down, gain_attn, gain_ffn = weights
-    group, cosine, sine, bias = place
-    normed, queries, kv_own = project(hidden, gain_attn, w_qkv, cosine, sine)
+    ids, group, cosine, sine, bias = place
+    normed, queries, kv_own = project(ids, hidden, gain_attn, w_qkv, cosine, sine)
     kv_all = jnp.concatenate(flip_gather(kv_own, group), axis=0)
     mixed, lse = attend_forward(queries, kv_all, bias)
-    middle, ffn_in = mix(mixed, w_out, hidden, gain_ffn)
-    inner, *slopes = gate_up(ffn_in, w_gate, w_up, tick != "a")
-    out, low = down(inner, w_down, middle)
+    middle, ffn_in = mix(ids, mixed, w_out, hidden, gain_ffn)
+    inner, *slopes = gate_up(ids, ffn_in, w_gate, w_up, tick != "a")
+    out, low = down(ids, inner, w_down, middle)
     return out, low, (hidden, normed, queries, kv_all, lse, mixed, middle, ffn_in, inner, slopes)
 
 
 def backward_layer(grad, kept, weights, place):
     w_qkv, w_out, w_gate, w_up, w_down, gain_attn, gain_ffn = weights
-    group, cosine, sine, bias = place
+    ids, group, cosine, sine, bias = place
     hidden, normed, queries, kv_all, lse, mixed, middle, ffn_in, inner, slopes = kept
-    d_gu = d_inner(grad, w_down, *slopes)
+    d_gu = d_inner(ids, grad, w_down, *slopes)
     d_mid, mid_low, d_mixed, gain_ffn_grad = d_middle(
-        d_gu, w_gate, w_up, middle, gain_ffn, grad, w_out
+        ids, d_gu, w_gate, w_up, middle, gain_ffn, grad, w_out
     )
     d_q, *d_kv = attend_backward(queries, kv_all, d_mixed, bias, lse, cosine, sine)
     dk, dk2 = flip_reduce(d_kv[0::2], group)
     dv, dv2 = flip_reduce(d_kv[1::2], group)
     d_kv, d_hid, hid_low, gain_attn_grad = d_hidden(
-        d_q, (dk, dv, dk2, dv2), cosine, sine, w_qkv, hidden, gain_attn, d_mid
+        ids, d_q, (dk, dv, dk2, dv2), cosine, sine, w_qkv, hidden, gain_attn, d_mid
     )
     pairs = {
         "d": (inner, (grad,)),
@@ -590,7 +780,7 @@
 
 
 def reduced(other, own, group):
-    return rep_sum(own + flip(other, group))
+    return rep_sum(plus(own, flip(other, group)))
 
 
 def shards(
@@ -643,18 +833,21 @@
     cosine = jnp.tile(jnp.cos(angles), (1, 4))
     sine = jnp.sin(angles)
     sine = jnp.concatenate([-sine, sine, -sine, sine], axis=1)
-    place = (group, cosine, sine, bias)
+    here = jnp.stack([me, lax.axis_index("rep")]).astype(jnp.int32)
+    place = (here, group, cosine, sine, bias)
 
     gains = flip_gather(jnp.stack([norm_attn[0], norm_ffn[0]]), count)
-    gains = put_rows(gains, [me ^ p for p in range(count)]).reshape(count, 2, -1)
-    gains = gains.transpose(1, 0, 2).reshape(2, 1, -1).astype(F32)
+    gain_table = jnp.zeros((count,) + gains[0].shape, BF16)
+    for p, piece in enumerate(gains):
+        gain_table = lax.dynamic_update_slice(gain_table, piece[None], (me ^ p, 0, 0))
+    gains = gain_table.transpose(1, 0, 2).reshape(2, 1, -1).astype(F32)
     qkv_shard = jnp.concatenate([w_query[0], w_key[0], w_value[0]], axis=1)
     weights = (
-        gather_rows(qkv_shard, count, me),
-        gather_rows(w_out[0], count, me),
-        gather_over_rep(w_gate[0], count, me),
-        gather_over_rep(w_up[0], count, me),
-        gather_rows(w_down[0], count, me),
+        row_pieces(qkv_shard, count),
+        row_pieces(w_out[0], count),
+        column_pieces(w_gate[0], count),
+        column_pieces(w_up[0], count),
+        row_pieces(w_down[0], count),
         gains[0],
         gains[1],
     )

time: 789 us -> 739 us (0.937)
  other arithmetic: 76.4 us -> 35.5 us
  Pallas kernels: 200 us -> 189 us
    unnamed x113 -> x271, local copies, waits for them, and re-layouts: 8.5 us -> 46.5 us
    dynamic_update_slice x30 -> x4, local copies, waits for them, and re-layouts: 38.1 us -> 3.02 us  [shards(): lax.dynamic_update_slice(gain_table, piece[None], (me ^ p, 0, 0))]
    add x27 -> x0, other arithmetic: 30.3 us -> none  [the longest x9 13.1 us: reduced(): return rep_sum(own + flip(other, group))]
    ppermute x47 -> x53, waiting for transfers between devices: 89.1 us -> 107 us  [flip(): lax.ppermute(block, axis, [(i, i ^ bit) for i in range(lax.axis_size(axis...]
    ppermute x24, waiting for transfers between devices: 133 us -> 119 us  [the longest x6 62.1 us: column_pieces(): lax.ppermute(part, 'rep', [(i, (i + k) % reps) for i in range(reps)])]
    pallas_call x9, Pallas kernels: 36.5 us -> 26 us  [grad_product(): kernel(grad_kernel, 4 * total * tokens * rows * cols, 8 * rows * cols, gr...]
    another operation x4 -> x0, local copies, waits for them, and re-layouts: 10.4 us -> none
    pallas_call x14 -> x41, Pallas kernels: 115 us -> 120 us  [the longest x2 25 us: d_middle(): kernel(body, 4 * rows * model * width + 2 * rows * model * WQ, 4 * model...]
  transfers between devices with their start and end apart: 84 -> 90, of which waited for: 27 -> 28; matrix products, arithmetic and copies ran while one was open for 19% -> 10% of each run, Pallas kernels for 24% -> 24%
where the time goes in v1:
time: 739 us; the launch traced here: 732 us
  waiting for transfers between devices  318 us (43%)
  Pallas kernels  189 us (26%)
  starting transfers between devices  104 us (14%)
  local copies, waits for them, and re-layouts  82.1 us (11%)
  other arithmetic  35.5 us (5%)
    ppermute x53, waiting for transfers between devices, flip(): lax.ppermute(block, axis, [(i, i ^ bit) for i in range(lax.axis_size(axis...  107 us
    ppermute x9, waiting for transfers between devices, rep_sum(): arrived = lax.ppermute(value, 'rep', [(1, 0), (2, 3)])  66.3 us
    ppermute x6, waiting for transfers between devices, column_pieces(): lax.ppermute(part, 'rep', [(i, (i + k) % reps) for i in range(reps)])  62.1 us
    ppermute x9, waiting for transfers between devices, rep_sum(): arrived = lax.ppermute(value, 'rep', [(0, 1), (3, 2)])  56.8 us
    unnamed x271, local copies, waits for them, and re-layouts  46.5 us
    ppermute x53, starting transfers between devices, flip(): lax.ppermute(block, axis, [(i, i ^ bit) for i in range(lax.axis_size(axis...  29.2 us
    pallas_call x9, Pallas kernels, grad_product(): kernel(grad_kernel, 4 * total * tokens * rows * cols, 8 * rows * cols, gr...  26 us
    ppermute x4, waiting for transfers between devices, shifted(): return lax.ppermute(block, axis, route)  26 us
  transfers between devices with their start and end apart: 90, of which 28 were waited for; matrix products, arithmetic and copies ran while one was open for 10% of the time, Pallas kernels for 24%

profile of v1, /device:TPU:0, one launch (start us, length us, event | category | flops | bytes accessed | tf_op | source)
XLA Modules:
  0.0 731.7 jit_solution(17903639855590048673)
XLA Ops:
  19.4 16.0 %collective-permute-done.22.rest_12_ = bf16[288,768]{1,0:T(8,128)(2,1)S(1)} collective-permute-done((bf16[288,768]{1,0:T(8,128)(2,1)S(1)}, bf16[288,768]{1,0:T(8,128)(2,1)S(1)}, u32[]{:S(2)}, u32[]{:S(2)}) %collective-permute-start.22) | collective-permute-done | bytes 442400 | tf_op jit(solution)/shard_map/ppermute | solution.py:26
  59.2 27.7 %collective-permute-done.24.rest_14_ = bf16[288,768]{1,0:T(8,128)(2,1)} collective-permute-done((bf16[288,768]{1,0:T(8,128)(2,1)S(1)}, bf16[288,768]{1,0:T(8,128)(2,1)}, u32[]{:S(2)}, u32[]{:S(2)}) %collective-permute-start.24) | collective-permute-done | bytes 442400 | tf_op jit(solution)/shard_map/ppermute | solution.py:69
  86.9 11.2 %collective-permute-start.15 = (bf16[288,768]{1,0:T(8,128)(2,1)}, bf16[288,768]{1,0:T(8,128)(2,1)}, u32[]{:S(2)}, u32[]{:S(2)}) collective-permute-start(bf16[288,768]{1,0:T(8,128)(2,1)} %collective-permute-done.13.rest_2_), channel_id=1, source_target_pairs={{0,2},{1,3},{2,0},{3,1},{4,6},{5,7},{6,4},{7,5},{8,10},{9,11},{10,... | collective-permute-start | bytes 1327112 | tf_op jit(solution)/shard_map/ppermute | solution.py:69
  99.4 18.8 %collective-permute-done.15.rest_4_ = bf16[288,768]{1,0:T(8,128)(2,1)} collective-permute-done((bf16[288,768]{1,0:T(8,128)(2,1)}, bf16[288,768]{1,0:T(8,128)(2,1)}, u32[]{:S(2)}, u32[]{:S(2)}) %collective-permute-start.15) | collective-permute-done | bytes 442400 | tf_op jit(solution)/shard_map/ppermute | solution.py:69
  118.8 13.5 %collective-permute-done.14.rest_3_ = bf16[288,768]{1,0:T(8,128)(2,1)} collective-permute-done((bf16[288,768]{1,0:T(8,128)(2,1)}, bf16[288,768]{1,0:T(8,128)(2,1)}, u32[]{:S(2)}, u32[]{:S(2)}) %collective-permute-start.14) | collective-permute-done | bytes 442400 | tf_op jit(solution)/shard_map/ppermute | solution.py:69
  173.3 10.3 %shard_map.204 = (bf16[256,1152]{1,0:T(8,128)(2,1)S(1)}, f32[3,8,256]{2,1,0:T(8,128)}) custom-call(bf16[256,1152]{1,0:T(8,128)(2,1)S(1)} %copy-done.97, bf16[512,768]{1,0:T(8,128)(2,1)S(1)} %pad_maximum_fusion.1.k_ref.v_ref, bf16[512,768]{1,0:T(8,128)(2,1)S(1)} %pad_maximum_fusion.1.k_ref.v_ref, f32[512,256]{1,0:T(8,128)S(1)} %copy-done.80), custom_call_target="tpu_custom_call" | custom-call | flops 1207959552 | bytes 4194304 | tf_op jit(solution)/shard_map/pallas_call | solution.py:273
  205.7 12.4 %collective-permute-done.33 = bf16[256,1152]{1,0:T(8,128)(2,1)} collective-permute-done((bf16[256,1152]{1,0:T(8,128)(2,1)}, bf16[256,1152]{1,0:T(8,128)(2,1)}, u32[]{:S(2)}, u32[]{:S(2)}) %collective-permute-start.33) | collective-permute-done | bytes 589856 | tf_op jit(solution)/shard_map/ppermute | solution.py:32
  233.1 9.8 %shard_map.209 = (bf16[256,1152]{1,0:T(8,128)(2,1)S(1)}, f32[3,8,256]{2,1,0:T(8,128)S(1)}) custom-call(bf16[256,1152]{1,0:T(8,128)(2,1)S(1)} %copy-done.92, bf16[512,768]{1,0:T(8,128)(2,1)S(1)} %constant_dynamic-update-slice_fusion.k_ref.v_ref, bf16[512,768]{1,0:T(8,128)(2,1)S(1)} %constant_dynamic-update-slice_fusion.k_ref.v_ref, f32[512,256]{1,0:T(8,128)S(1)} %copy-done.81), custom_call_target="tpu_custom_call" | custom-call | flops 1207959552 | bytes 4194304 | tf_op jit(solution)/shard_map/pallas_call | solution.py:273
  292.6 13.1 %shard_map.214 = (f32[256,1152]{1,0:T(8,128)S(1)}, bf16[256,1152]{1,0:T(8,128)(2,1)}, bf16[256,1152]{1,0:T(8,128)(2,1)S(1)}, f32[1,1152]{1,0:T(1,128)}) custom-call(s32[2]{0:T(128)S(1)} %pad_add_fusion.2.ids_ref, bf16[2,256,3072]{2,1,0:T(8,128)(2,1)} %copy-done.19, f32[256,1152]{1,0:T(8,128)S(1)} %copy-done.21, f32[1,1152]{1,0:T(1,128)S(1)} %copy-done.90, ...), custom_call_target="tpu_custom_call" | custom-call | flops 4303355904 | bytes 20840448 | tf_op jit(solution)/shard_map/pallas_call | solution.py:608
  305.8 11.2 %shard_map.215 = (bf16[256,1152]{1,0:T(8,128)(2,1)S(1)}, bf16[256,384]{1,0:T(8,128)(2,1)S(1)}, bf16[256,384]{1,0:T(8,128)(2,1)S(1)}, bf16[256,384]{1,0:T(8,128)(2,1)S(1)}, bf16[256,384]{1,0:T(8,128)(2,1)S(1)}) custom-call(bf16[256,1152]{1,0:T(8,128)(2,1)S(1)} %copy-done.93, bf16[512,768]{1,0:T(8,128)(2,1)S(1)} %copy-done.87, ...), custom_call_target="tpu_custom_call" | custom-call | flops 2415919104 | bytes 8388608 | tf_op jit(solution)/shard_map/pallas_call | solution.py:336
  336.2 12.9 %collective-permute-done.39 = bf16[256,1152]{1,0:T(8,128)(2,1)S(1)} collective-permute-done((bf16[256,1152]{1,0:T(8,128)(2,1)S(1)}, bf16[256,1152]{1,0:T(8,128)(2,1)S(1)}, u32[]{:S(2)}, u32[]{:S(2)}) %collective-permute-start.39) | collective-permute-done | bytes 589856 | tf_op jit(solution)/shard_map/ppermute | solution.py:32
  357.6 11.9 %shard_map.218 = (f32[256,1152]{1,0:T(8,128)S(1)}, bf16[256,1152]{1,0:T(8,128)(2,1)S(1)}, bf16[256,1152]{1,0:T(8,128)(2,1)S(1)}, f32[1,1152]{1,0:T(1,128)S(1)}) custom-call(s32[2]{0:T(128)S(1)} %pad_add_fusion.2.ids_ref, bf16[2,256,3072]{2,1,0:T(8,128)(2,1)} %copy-done.2, f32[256,1152]{1,0:T(8,128)S(1)} %copy-done.21, f32[1,1152]{1,0:T(1,128)S(1)} %copy-done.90, ...), custom_call_target="tpu_custom_call" | custom-call | flops 4303355904 | bytes 20840448 | tf_op jit(solution)/shard_map/pallas_call | solution.py:608
  369.5 11.8 %shard_map.219 = (bf16[256,1152]{1,0:T(8,128)(2,1)}, bf16[256,384]{1,0:T(8,128)(2,1)S(1)}, bf16[256,384]{1,0:T(8,128)(2,1)S(1)}, bf16[256,384]{1,0:T(8,128)(2,1)S(1)}, bf16[256,384]{1,0:T(8,128)(2,1)S(1)}) custom-call(bf16[256,1152]{1,0:T(8,128)(2,1)S(1)} %copy-done.93, bf16[512,768]{1,0:T(8,128)(2,1)S(1)} %copy-done.87, bf16[512,768]{1,0:T(8,128)(2,1)S(1)} %copy-done.87, ...), custom_call_target="tpu_custom_call" | custom-call | flops 2415919104 | bytes 8388608 | tf_op jit(solution)/shard_map/pallas_call | solution.py:336
  430.9 32.5 %collective-permute-done.52.right_ref = bf16[288,896]{1,0:T(8,128)(2,1)S(1)} collective-permute-done((bf16[288,896]{1,0:T(8,128)(2,1)S(1)}, bf16[288,896]{1,0:T(8,128)(2,1)S(1)}, u32[]{:S(2)}, u32[]{:S(2)}) %collective-permute-start.52) | collective-permute-done | bytes 516128 | tf_op jit(solution)/shard_map/ppermute | solution.py:26
  467.9 14.5 %collective-permute-done.86.right_ref = bf16[384,1152]{1,0:T(8,128)(2,1)S(1)} collective-permute-done((bf16[384,1152]{1,0:T(8,128)(2,1)S(1)}, bf16[384,1152]{1,0:T(8,128)(2,1)S(1)}, u32[]{:S(2)}, u32[]{:S(2)}) %collective-permute-start.86) | collective-permute-done | bytes 884768 | tf_op jit(solution)/shard_map/ppermute | solution.py:26
  485.3 14.8 %collective-permute-done.82.right_ref = bf16[384,1152]{1,0:T(8,128)(2,1)S(1)} collective-permute-done((bf16[384,1152]{1,0:T(8,128)(2,1)S(1)}, bf16[384,1152]{1,0:T(8,128)(2,1)S(1)}, u32[]{:S(2)}, u32[]{:S(2)}) %collective-permute-start.82) | collective-permute-done | bytes 884768 | tf_op jit(solution)/shard_map/ppermute | solution.py:26
  515.4 10.5 %collective-permute-done.87.right_ref = bf16[384,1152]{1,0:T(8,128)(2,1)S(1)} collective-permute-done((bf16[384,1152]{1,0:T(8,128)(2,1)S(1)}, bf16[384,1152]{1,0:T(8,128)(2,1)S(1)}, u32[]{:S(2)}, u32[]{:S(2)}) %collective-permute-start.87) | collective-permute-done | bytes 884768 | tf_op jit(solution)/shard_map/ppermute | solution.py:125
  607.4 12.1 %collective-permute-done.73.right_ref = bf16[288,1536]{1,0:T(8,128)(2,1)S(1)} collective-permute-done((bf16[288,1536]{1,0:T(8,128)(2,1)S(1)}, bf16[288,1536]{1,0:T(8,128)(2,1)S(1)}, u32[]{:S(2)}, u32[]{:S(2)}) %collective-permute-start.73) | collective-permute-done | bytes 884768 | tf_op jit(solution)/shard_map/ppermute | solution.py:125
  622.3 16.1 %collective-permute-done.69.right_ref = bf16[288,1536]{1,0:T(8,128)(2,1)S(1)} collective-permute-done((bf16[288,1536]{1,0:T(8,128)(2,1)S(1)}, bf16[288,1536]{1,0:T(8,128)(2,1)S(1)}, u32[]{:S(2)}, u32[]{:S(2)}) %collective-permute-start.69) | collective-permute-done | bytes 884768 | tf_op jit(solution)/shard_map/ppermute | solution.py:125
  639.2 12.5 %collective-permute-done.65.right_ref = bf16[288,1536]{1,0:T(8,128)(2,1)S(1)} collective-permute-done((bf16[288,1536]{1,0:T(8,128)(2,1)S(1)}, bf16[288,1536]{1,0:T(8,128)(2,1)S(1)}, u32[]{:S(2)}, u32[]{:S(2)}) %collective-permute-start.65) | collective-permute-done | bytes 884768 | tf_op jit(solution)/shard_map/ppermute | solution.py:125
  660.4 18.1 %collective-permute-done.79 = bf16[288,1536]{1,0:T(8,128)(2,1)S(1)} collective-permute-done((bf16[288,1536]{1,0:T(8,128)(2,1)S(1)}, bf16[288,1536]{1,0:T(8,128)(2,1)S(1)}, u32[]{:S(2)}, u32[]{:S(2)}) %collective-permute-start.79) | collective-permute-done | bytes 884768 | tf_op jit(solution)/shard_map/ppermute | solution.py:129
  678.5 18.9 %collective-permute-done.75 = bf16[288,1536]{1,0:T(8,128)(2,1)S(1)} collective-permute-done((bf16[288,1536]{1,0:T(8,128)(2,1)S(1)}, bf16[288,1536]{1,0:T(8,128)(2,1)S(1)}, u32[]{:S(2)}, u32[]{:S(2)}) %collective-permute-start.75) | collective-permute-done | bytes 884768 | tf_op jit(solution)/shard_map/ppermute | solution.py:129
  699.7 16.6 %collective-permute-done.71 = bf16[288,1536]{1,0:T(8,128)(2,1)S(1)} collective-permute-done((bf16[288,1536]{1,0:T(8,128)(2,1)S(1)}, bf16[288,1536]{1,0:T(8,128)(2,1)S(1)}, u32[]{:S(2)}, u32[]{:S(2)}) %collective-permute-start.71) | collective-permute-done | bytes 884768 | tf_op jit(solution)/shard_map/ppermute | solution.py:129
  716.5 12.7 %collective-permute-done.67 = bf16[288,1536]{1,0:T(8,128)(2,1)S(1)} collective-permute-done((bf16[288,1536]{1,0:T(8,128)(2,1)S(1)}, bf16[288,1536]{1,0:T(8,128)(2,1)S(1)}, u32[]{:S(2)}, u32[]{:S(2)}) %collective-permute-start.67) | collective-permute-done | bytes 884768 | tf_op jit(solution)/shard_map/ppermute | solution.py:129
  (567 shorter events, 368.3 us)
Async XLA Ops:
  7.9 46.2 %collective-permute-start.10 = (bf16[288,1152]{1,0:T(8,128)(2,1)}, bf16[288,1152]{1,0:T(8,128)(2,1)}, u32[]{:S(2)}, u32[]{:S(2)}) collective-permute-start(bf16[288,1152]{1,0:T(8,128)(2,1)} %bitcast.121), channel_id=1, source_target_pairs={{0,8},{4,12},{8,0},{12,4},{1,9},{5,13},{9,1},{13,5},{2,10},{6,14},... | collective-permute-start | bytes 1990664 | tf_op jit(solution)/shard_map/ppermute | solution.py:26
  8.5 46.3 %collective-permute-start.9 = (bf16[288,1152]{1,0:T(8,128)(2,1)}, bf16[288,1152]{1,0:T(8,128)(2,1)}, u32[]{:S(2)}, u32[]{:S(2)}) collective-permute-start(bf16[288,1152]{1,0:T(8,128)(2,1)} %bitcast.122), channel_id=1, source_target_pairs={{0,4},{4,0},{8,12},{12,8},{1,5},{5,1},{9,13},{13,9},{2,6},{6,2},{1... | collective-permute-start | bytes 1990664 | tf_op jit(solution)/shard_map/ppermute | solution.py:26
  54.2 64.0 %collective-permute-start.6 = (bf16[288,1920]{1,0:T(8,128)(2,1)}, bf16[288,1920]{1,0:T(8,128)(2,1)}, u32[]{:S(2)}, u32[]{:S(2)}) collective-permute-start(bf16[288,1920]{1,0:T(8,128)(2,1)} %pad_maximum_fusion.rest_0_), channel_id=1, source_target_pairs={{0,8},{4,12},{8,0},{12,4},{1,9},{5,13},{9,1},{13,5},{2,10},{6,14},... | collective-permute-start | bytes 3317768 | tf_op jit(solution)/shard_map/ppermute | solution.py:26
  59.2 73.2 %collective-permute-start.5 = (bf16[288,1920]{1,0:T(8,128)(2,1)}, bf16[288,1920]{1,0:T(8,128)(2,1)}, u32[]{:S(2)}, u32[]{:S(2)}) collective-permute-start(bf16[288,1920]{1,0:T(8,128)(2,1)} %pad_maximum_fusion.rest_0_), channel_id=1, source_target_pairs={{0,4},{4,0},{8,12},{12,8},{1,5},{5,1},{9,13},{13,9},{2,6},{6,2},{1... | collective-permute-start | bytes 3317768 | tf_op jit(solution)/shard_map/ppermute | solution.py:26
  98.8 53.2 %collective-permute-start.31 = (bf16[768,1152]{1,0:T(8,128)(2,1)}, bf16[768,1152]{1,0:T(8,128)(2,1)}, u32[]{:S(2)}, u32[]{:S(2)}) collective-permute-start(bf16[768,1152]{1,0:T(8,128)(2,1)} %bitcast.21.rest_0_), channel_id=1, source_target_pairs={{0,8},{4,12},{8,0},{12,4},{1,9},{5,13},{9,1},{13,5},{2,10},{6,14},... | collective-permute-start | bytes 5308424 | tf_op jit(solution)/shard_map/ppermute | solution.py:26
  137.6 49.7 %collective-permute-start.12 = (bf16[288,3072]{1,0:T(8,128)(2,1)S(1)}, bf16[288,3072]{1,0:T(8,128)(2,1)}, u32[]{:S(2)}, u32[]{:S(2)}) collective-permute-start(bf16[288,3072]{1,0:T(8,128)(2,1)S(1)} %bitcast.111), channel_id=1, source_target_pairs={{0,4},{4,0},{8,12},{12,8},{1,5},{5,1},{9,13},{13,9},{2,6},{6,2},{1... | collective-permute-start | bytes 5308424 | tf_op jit(solution)/shard_map/ppermute | solution.py:26
  138.6 48.8 %collective-permute-start.21 = (bf16[288,3072]{1,0:T(8,128)(2,1)S(1)}, bf16[288,3072]{1,0:T(8,128)(2,1)}, u32[]{:S(2)}, u32[]{:S(2)}) collective-permute-start(bf16[288,3072]{1,0:T(8,128)(2,1)S(1)} %bitcast.116), channel_id=1, source_target_pairs={{0,4},{4,0},{8,12},{12,8},{1,5},{5,1},{9,13},{13,9},{2,6},{6,2},{1... | collective-permute-start | bytes 5308424 | tf_op jit(solution)/shard_map/ppermute | solution.py:26
  151.8 44.1 %collective-permute-start.30 = (bf16[768,1152]{1,0:T(8,128)(2,1)}, bf16[768,1152]{1,0:T(8,128)(2,1)}, u32[]{:S(2)}, u32[]{:S(2)}) collective-permute-start(bf16[768,1152]{1,0:T(8,128)(2,1)} %bitcast.21.rest_0_), channel_id=1, source_target_pairs={{0,4},{4,0},{8,12},{12,8},{1,5},{5,1},{9,13},{13,9},{2,6},{6,2},{1... | collective-permute-start | bytes 5308424 | tf_op jit(solution)/shard_map/ppermute | solution.py:26
  152.4 43.5 %collective-permute-start.32 = (bf16[768,1152]{1,0:T(8,128)(2,1)}, bf16[768,1152]{1,0:T(8,128)(2,1)}, u32[]{:S(2)}, u32[]{:S(2)}) collective-permute-start(bf16[768,1152]{1,0:T(8,128)(2,1)} %collective-permute-done.31.rest_2_), channel_id=1, source_target_pairs={{0,4},{4,0},{8,12},{12,8},{1,5},{5,1},{9,13},{13,9},{2,6},{6,2},{1... | collective-permute-start | bytes 5308424 | tf_op jit(solution)/shard_map/ppermute | solution.py:26
  231.8 164.3 %collective-permute-start.44 = (bf16[576,256]{1,0:T(8,128)(2,1)}, bf16[576,256]{1,0:T(8,128)(2,1)}, u32[]{:S(2)}, u32[]{:S(2)}) collective-permute-start(bf16[576,256]{1,0:T(8,128)(2,1)} %pad_maximum_fusion.8), channel_id=1, source_target_pairs={{0,4},{4,0},{8,12},{12,8},{1,5},{5,1},{9,13},{13,9},{2,6},{6,2},{1... | collective-permute-start | bytes 884744 | tf_op jit(solution)/shard_map/ppermute | solution.py:26
  249.1 147.0 %collective-permute-start.56 = (bf16[576,256]{1,0:T(8,128)(2,1)}, bf16[576,256]{1,0:T(8,128)(2,1)}, u32[]{:S(2)}, u32[]{:S(2)}) collective-permute-start(bf16[576,256]{1,0:T(8,128)(2,1)} %pad_maximum_fusion.10), channel_id=1, source_target_pairs={{0,4},{4,0},{8,12},{12,8},{1,5},{5,1},{9,13},{13,9},{2,6},{6,2},{1... | collective-permute-start | bytes 884744 | tf_op jit(solution)/shard_map/ppermute | solution.py:26
  323.7 58.1 %collective-permute-start.35 = (bf16[128,1152]{1,0:T(8,128)(2,1)S(1)}, bf16[128,1152]{1,0:T(8,128)(2,1)S(1)}, u32[]{:S(2)}, u32[]{:S(2)}) collective-permute-start(bf16[128,1152]{1,0:T(8,128)(2,1)S(1)} %slice.107), channel_id=1, source_target_pairs={{0,8},{4,12},{8,0},{12,4},{1,9},{5,13},{9,1},{13,5},{2,10},{6,14},... | collective-permute-start | bytes 884744 | tf_op jit(solution)/shard_map/ppermute | solution.py:26
  391.7 113.9 %collective-permute-start.63 = (bf16[2,256,3072]{2,1,0:T(8,128)(2,1)S(1)}, bf16[2,256,3072]{2,1,0:T(8,128)(2,1)}, u32[]{:S(2)}, u32[]{:S(2)}) collective-permute-start(bf16[2,256,3072]{2,1,0:T(8,128)(2,1)S(1)} %copy-done.3), channel_id=1, source_target_pairs={{0,4},{4,0},{8,12},{12,8},{1,5},{5,1},{9,13},{13,9},{2,6},{6,2},{1... | collective-permute-start | bytes 9437192 | tf_op jit(solution)/shard_map/ppermute | solution.py:26
  420.4 44.6 %collective-permute-start.58 = (bf16[288,1152]{1,0:T(8,128)(2,1)S(1)}, bf16[288,1152]{1,0:T(8,128)(2,1)S(1)}, u32[]{:S(2)}, u32[]{:S(2)}) collective-permute-start(bf16[288,1152]{1,0:T(8,128)(2,1)S(1)} %get-tuple-element.108), channel_id=1, source_target_pairs={{0,8},{4,12},{8,0},{12,4},{1,9},{5,13},{9,1},{13,5},{2,10},{6,14},... | collective-permute-start | bytes 1990664 | tf_op jit(solution)/shard_map/ppermute | solution.py:26
  421.8 44.6 %collective-permute-start.46 = (bf16[288,1152]{1,0:T(8,128)(2,1)S(1)}, bf16[288,1152]{1,0:T(8,128)(2,1)S(1)}, u32[]{:S(2)}, u32[]{:S(2)}) collective-permute-start(bf16[288,1152]{1,0:T(8,128)(2,1)S(1)} %get-tuple-element.100), channel_id=1, source_target_pairs={{0,8},{4,12},{8,0},{12,4},{1,9},{5,13},{9,1},{13,5},{2,10},{6,14},... | collective-permute-start | bytes 1990664 | tf_op jit(solution)/shard_map/ppermute | solution.py:26
  422.4 41.0 %collective-permute-start.52 = (bf16[288,896]{1,0:T(8,128)(2,1)S(1)}, bf16[288,896]{1,0:T(8,128)(2,1)S(1)}, u32[]{:S(2)}, u32[]{:S(2)}) collective-permute-start(bf16[288,896]{1,0:T(8,128)(2,1)S(1)} %fusion.15), channel_id=1, source_target_pairs={{0,8},{4,12},{8,0},{12,4},{1,9},{5,13},{9,1},{13,5},{2,10},{6,14},... | collective-permute-start | bytes 1548296 | tf_op jit(solution)/shard_map/ppermute | solution.py:26
  427.4 55.0 %collective-permute-start.86 = (bf16[384,1152]{1,0:T(8,128)(2,1)S(1)}, bf16[384,1152]{1,0:T(8,128)(2,1)S(1)}, u32[]{:S(2)}, u32[]{:S(2)}) collective-permute-start(bf16[384,1152]{1,0:T(8,128)(2,1)S(1)} %get-tuple-element.120), channel_id=1, source_target_pairs={{0,8},{4,12},{8,0},{12,4},{1,9},{5,13},{9,1},{13,5},{2,10},{6,14},... | collective-permute-start | bytes 2654216 | tf_op jit(solution)/shard_map/ppermute | solution.py:26
  483.9 42.0 %collective-permute-start.87 = (bf16[384,1152]{1,0:T(8,128)(2,1)S(1)}, bf16[384,1152]{1,0:T(8,128)(2,1)S(1)}, u32[]{:S(2)}, u32[]{:S(2)}) collective-permute-start(bf16[384,1152]{1,0:T(8,128)(2,1)S(1)} %shard_map.254.left_ref), channel_id=1, source_target_pairs={{0,1},{3,2},{4,5},{7,6},{8,9},{11,10},{12,13},{15,14},{16,17},{19,... | collective-permute-start | bytes 2654216 | tf_op jit(solution)/shard_map/ppermute | solution.py:125
  510.6 48.6 %collective-permute-start.76 = (bf16[288,1536]{1,0:T(8,128)(2,1)}, bf16[288,1536]{1,0:T(8,128)(2,1)}, u32[]{:S(2)}, u32[]{:S(2)}) collective-permute-start(bf16[288,1536]{1,0:T(8,128)(2,1)} %get-tuple-element.116), channel_id=1, source_target_pairs={{0,8},{4,12},{8,0},{12,4},{1,9},{5,13},{9,1},{13,5},{2,10},{6,14},... | collective-permute-start | bytes 2654216 | tf_op jit(solution)/shard_map/ppermute | solution.py:26
  599.6 54.4 %collective-permute-start.85 = (bf16[384,1152]{1,0:T(8,128)(2,1)S(1)}, bf16[384,1152]{1,0:T(8,128)(2,1)S(1)}, u32[]{:S(2)}, u32[]{:S(2)}) collective-permute-start(bf16[384,1152]{1,0:T(8,128)(2,1)S(1)} %shard_map.252), channel_id=1, source_target_pairs={{1,0},{2,3},{5,4},{6,7},{9,8},{10,11},{13,12},{14,15},{17,16},{18,... | collective-permute-start | bytes 2654216 | tf_op jit(solution)/shard_map/ppermute | solution.py:129
  606.0 45.8 %collective-permute-start.65 = (bf16[288,1536]{1,0:T(8,128)(2,1)S(1)}, bf16[288,1536]{1,0:T(8,128)(2,1)S(1)}, u32[]{:S(2)}, u32[]{:S(2)}) collective-permute-start(bf16[288,1536]{1,0:T(8,128)(2,1)S(1)} %shard_map.234.left_ref), channel_id=1, source_target_pairs={{0,1},{3,2},{4,5},{7,6},{8,9},{11,10},{12,13},{15,14},{16,17},{19,... | collective-permute-start | bytes 2654216 | tf_op jit(solution)/shard_map/ppermute | solution.py:125
  654.2 43.2 %collective-permute-start.75 = (bf16[288,1536]{1,0:T(8,128)(2,1)S(1)}, bf16[288,1536]{1,0:T(8,128)(2,1)S(1)}, u32[]{:S(2)}, u32[]{:S(2)}) collective-permute-start(bf16[288,1536]{1,0:T(8,128)(2,1)S(1)} %shard_map.244), channel_id=1, source_target_pairs={{1,0},{2,3},{5,4},{6,7},{9,8},{10,11},{13,12},{14,15},{17,16},{18,... | collective-permute-start | bytes 2654216 | tf_op jit(solution)/shard_map/ppermute | solution.py:129
  657.7 58.7 %collective-permute-start.71 = (bf16[288,1536]{1,0:T(8,128)(2,1)S(1)}, bf16[288,1536]{1,0:T(8,128)(2,1)S(1)}, u32[]{:S(2)}, u32[]{:S(2)}) collective-permute-start(bf16[288,1536]{1,0:T(8,128)(2,1)S(1)} %shard_map.240), channel_id=1, source_target_pairs={{1,0},{2,3},{5,4},{6,7},{9,8},{10,11},{13,12},{14,15},{17,16},{18,... | collective-permute-start | bytes 2654216 | tf_op jit(solution)/shard_map/ppermute | solution.py:129
  659.1 70.1 %collective-permute-start.67 = (bf16[288,1536]{1,0:T(8,128)(2,1)S(1)}, bf16[288,1536]{1,0:T(8,128)(2,1)S(1)}, u32[]{:S(2)}, u32[]{:S(2)}) collective-permute-start(bf16[288,1536]{1,0:T(8,128)(2,1)S(1)} %shard_map.236), channel_id=1, source_target_pairs={{1,0},{2,3},{5,4},{6,7},{9,8},{10,11},{13,12},{14,15},{17,16},{18,... | collective-permute-start | bytes 2654216 | tf_op jit(solution)/shard_map/ppermute | solution.py:129
  (199 other events, 2593.1 us)
